TPU v7x, 256 devices: a whole 4x4x8 slice. The times are simulated.
256 devices in a mesh: sa: 2 (over y_lo), gx: 16 (over z, core), gy: 8 (over x, y_hi).
Axes of the slice: x: 4, y: 4 (y_hi: 2, y_lo: 2; y = y_hi * 2 + y_lo), z: 8, core: 2. Of those that a mesh axis runs over, the one named last changes fastest.
Arguments:
- pred_frames: float32 [12, 32768], P(None, ('sa', 'gx', 'gy')), parts along dimension 1, may hold values from -52 to 52, as said below
- true_frames: float32 [12, 32768], P(None, ('sa', 'gx', 'gy')), parts along dimension 1, may hold values from -52 to 52, as said below
- pred_atoms: float32 [3, 57344], P(None, ('sa', 'gx', 'gy')), parts along dimension 1, may hold values from -52 to 52
- true_atoms: float32 [3, 57344], P(None, ('sa', 'gx', 'gy')), parts along dimension 1, may hold values from -52 to 52
- atom_mask: int32 [57344], P(('sa', 'gx', 'gy')), parts along dimension 0, may hold values from 0 to 1, as said below
- residue_types: int32 [4096], P(('sa', 'gx', 'gy')), parts along dimension 0, may hold values from 0 to 19
- swap_flags: int32 [4096], P(('sa', 'gx', 'gy')), parts along dimension 0, may hold values from 0 to 1
Outputs:
- frame_loss: float32 [32768], P(('sa', 'gx', 'gy')), parts along dimension 0
- atom_loss: float32 [57344], P(('sa', 'gx', 'gy')), parts along dimension 0
- total_loss: float32 [2], P('sa'), parts along dimension 0
There are 2 independent parts, one for each index of `sa`. A program takes and returns all parts, laid end to end along the dimension named above; each array names one. Nothing has to cross between parts.
Inputs may be any that keep to these rules, and one draw needn't show every extreme that they name: `atom_mask`: atom slots 0 to 3 of every residue, its backbone atoms, are 1. `pred_frames`: rows 0 to 8 of each frame hold a rotation matrix, row-major; rows 9 to 11 its translation. `true_frames`: rows 0 to 8 of each frame hold a rotation matrix, row-major; rows 9 to 11 its translation.
All inputs are finite; a program needn't handle non-finite values.
Results may differ from a plain program's by a relative error of at most 0.0001.
Values sent between devices are 32-bit elements; how exact they have to be, the bound alone decides.
A program may use at most 64 MiB of HBM per device.

v0:
```python
import functools
import math

import jax
import jax.numpy as jnp
import numpy as np
from jax import lax
from jax.sharding import Mesh
from jax.sharding import PartitionSpec as P

GY = ("gy_0", "gy_1")
GX = ("gx_0", "gx_1")
GX_GY = ("gx_0", "gx_1", "gy_0", "gy_1")
SA_GX_GY = ("sa", "gx_0", "gx_1", "gy_0", "gy_1")


eps_square = 0.0001
clamp_length = 10.0


def side_by_side(arrays, axis, dim, along):
    widths = [a.shape[along] for a in arrays]
    both = jnp.concatenate(arrays, axis=along)
    result = lax.all_gather(both, axis, axis=dim, tiled=True)
    return tuple(jnp.split(result, [sum(widths[:k]) for k in range(1, len(widths))], axis=along))


def gather_turned(arrays, axis, dims):
    turned = [jnp.moveaxis(a, dim, 0) for a, dim in zip(arrays, dims)]
    both = jnp.concatenate([t.reshape(len(t), -1) for t in turned], axis=1)
    result, at, gathered = (lax.all_gather(both, axis, axis=0, tiled=True), 0, [])
    for t, dim in zip(turned, dims):
        piece = result[:, at : at + t[0].size].reshape(-1, *t.shape[1:])
        gathered.append(jnp.moveaxis(piece, 0, dim))
        at += t[0].size
    return tuple(gathered)


def split_up(value, dim, length):
    lengths = value.shape
    tiles = value.reshape(*lengths[:dim], length, lengths[dim] // length, *lengths[dim + 1 :])
    return jnp.moveaxis(tiles, dim, 0)


def sent_and_summed(value, axis, dim):
    tiles = split_up(value, dim, lax.axis_size(axis))
    arrived = lax.all_to_all(tiles, axis, split_axis=0, concat_axis=0, tiled=True)
    return arrived.sum(axis=0)


def by_axis(value, axes):
    return functools.reduce(lax.psum, axes, value)


def residue_tables():
    atom_counts = np.array([5, 11, 8, 8, 6, 9, 9, 4, 10, 8, 8, 9, 8, 11, 7, 6, 7, 14, 12, 7])
    chi_counts = np.array([0, 4, 2, 2, 1, 3, 3, 0, 2, 2, 2, 4, 3, 2, 2, 1, 1, 2, 2, 1])
    atom_table = (np.arange(14)[None, :] < atom_counts[:, None]).astype(np.float32)
    slot_ids = np.arange(8)[None, :]
    frame_table = (
        (slot_ids == 0) | (slot_ids == 3) | (slot_ids >= 4) & (slot_ids - 3 <= chi_counts[:, None])
    ).astype(np.float32)
    partner_table = np.tile(np.arange(14), (20, 1))
    for restype, swap_pairs in (
        (3, ((6, 7),)),
        (6, ((7, 8),)),
        (13, ((6, 7), (8, 9))),
        (18, ((6, 7), (8, 9))),
    ):
        for first_slot, second_slot in swap_pairs:
            partner_table[restype, first_slot] = second_slot
            partner_table[restype, second_slot] = first_slot
    flip_table = np.zeros((20, 8), np.float32)
    flip_table[3, 5] = 1.0
    flip_table[13, 5] = 1.0
    flip_table[18, 5] = 1.0
    flip_table[6, 6] = 1.0
    sign_table = np.array([1, -1, -1, 1, -1, -1, 1, -1, -1, 1, 1, 1], np.float32)
    return (atom_table, frame_table, partner_table, flip_table, sign_table)


def type_onehot(residue_types):
    return residue_types[:, None] == jnp.arange(20, dtype=jnp.int32)[None, :]


def frame_terms(pred_frames, true_frames, residue_types, swap_flags):
    tables = residue_tables()
    onehot = type_onehot(residue_types).astype(jnp.float32)
    frame_table = jnp.asarray(tables[1], dtype=jnp.float32)
    flip_table = jnp.asarray(tables[3], dtype=jnp.float32)
    sign_table = jnp.asarray(tables[4], dtype=jnp.float32)
    exists = jnp.sum(onehot[:, :, None] * frame_table[None], axis=1)
    flips = jnp.sum(onehot[:, :, None] * flip_table[None], axis=1) * swap_flags[:, None].astype(
        jnp.float32
    )
    residues = residue_types.shape[0]
    shaped = true_frames.reshape(12, residues, 8)
    resolved = jnp.where(flips[None] > 0.5, shaped * sign_table[:, None, None], shaped).reshape(
        12, residues * 8
    )
    rot_pred = pred_frames[:9]
    rot_true = resolved[:9]
    offsets = []
    for column in range(3):
        true_part = (
            rot_true[column] * resolved[9]
            + rot_true[3 + column] * resolved[10]
            + rot_true[6 + column] * resolved[11]
        )
        pred_part = (
            rot_pred[column] * pred_frames[9]
            + rot_pred[3 + column] * pred_frames[10]
            + rot_pred[6 + column] * pred_frames[11]
        )
        offsets.append(true_part - pred_part)
    return (rot_pred, rot_true, jnp.stack(offsets, axis=0), exists.reshape(residues * 8))


def atom_terms(true_atoms, atom_mask, residue_types, swap_flags):
    tables = residue_tables()
    onehot_int = type_onehot(residue_types).astype(jnp.int32)
    onehot = onehot_int.astype(jnp.float32)
    partner_table = jnp.asarray(tables[2], dtype=jnp.int32)
    atom_table = jnp.asarray(tables[0], dtype=jnp.float32)
    partners = jnp.sum(onehot_int[:, :, None] * partner_table[None], axis=1)
    own_slots = jnp.broadcast_to(jnp.arange(14, dtype=jnp.int32)[None, :], partners.shape)
    source = jnp.where(swap_flags[:, None] == 1, partners, own_slots)
    residues = residue_types.shape[0]
    shaped = true_atoms.reshape(3, residues, 14)
    resolved = jnp.take_along_axis(
        shaped, jnp.broadcast_to(source[None], shaped.shape), axis=2
    ).reshape(3, residues * 14)
    mask_resolved = jnp.take_along_axis(atom_mask.reshape(residues, 14), source, axis=1)
    exists = jnp.sum(onehot[:, :, None] * atom_table[None], axis=1)
    weight = (exists * mask_resolved.astype(jnp.float32)).reshape(residues * 14)
    return (resolved, weight)


def clamped_errors(frame_side, atom_side):
    rot_pred, rot_true, offset = frame_side
    pred_pos, true_pos = atom_side
    squares = jnp.zeros((offset.shape[1], pred_pos.shape[1]), jnp.float32)
    for column in range(3):
        error = offset[column][:, None]
        for axis_row in range(3):
            error = error + rot_pred[3 * axis_row + column][:, None] * pred_pos[axis_row][None, :]
            error = error - rot_true[3 * axis_row + column][:, None] * true_pos[axis_row][None, :]
        squares = squares + error * error
    return jnp.minimum(jnp.sqrt(squares + eps_square), clamp_length) / clamp_length


def block_groups(shard_count, shard_cols, pair_limit):
    groups = max(1, min(shard_count, pair_limit // shard_cols))
    while shard_count % groups:
        groups -= 1
    lane_step = 128 // math.gcd(shard_cols, 128)
    return groups


def pair_folder(frame_side, row_exists, shard_cols):
    frame_rows = row_exists.shape[0]
    pair_limit = max(shard_cols, (1 << 20) // frame_rows)

    def add_pairs(carry, pieces, start):
        length = pieces[0].shape[1]
        block_width = length
        shard_count = length // shard_cols
        block_width = block_groups(shard_count, shard_cols, pair_limit) * shard_cols
        turn_count = length // block_width

        def one_block(turn_index, running):
            frame_raw, atom_sum = running
            begin_at = turn_index * block_width
            pred_block = lax.dynamic_slice_in_dim(pieces[0], begin_at, block_width, 1)
            true_block = lax.dynamic_slice_in_dim(pieces[1], begin_at, block_width, 1)
            weight_block = lax.dynamic_slice_in_dim(pieces[2], begin_at, block_width, 1)
            clamped = clamped_errors(frame_side, (pred_block, true_block))
            frame_raw = frame_raw + jnp.sum(clamped * weight_block, axis=1)
            column_sums = jnp.sum(clamped * row_exists[:, None], axis=0)
            atom_sum = lax.dynamic_update_slice_in_dim(atom_sum, column_sums, begin_at, 0)
            return (frame_raw, atom_sum)

        return lax.fori_loop(0, turn_count, one_block, carry)

    return add_pairs


def shards(pred_frames, true_frames, pred_atoms, true_atoms, atom_mask, residue_types, swap_flags):
    rot_pred, rot_true, offset, exists = frame_terms(
        pred_frames, true_frames, residue_types, swap_flags
    )
    true_resolved, weight = atom_terms(true_atoms, atom_mask, residue_types, swap_flags)
    shard_cols = pred_atoms.shape[1]
    rows = side_by_side((rot_pred, rot_true, offset, exists[None, :]), GY, 1, 0)
    row_exists = rows[3][0]
    folder = pair_folder((rows[0], rows[1], rows[2]), row_exists, shard_cols)
    start_state = (
        jnp.zeros(row_exists.shape, jnp.float32),
        jnp.zeros((shard_cols * lax.axis_size(GX),), jnp.float32),
    )
    row_raw, column_sum = folder(
        start_state,
        gather_turned((pred_atoms, true_resolved, weight[None, :]), GX, (1, 1, 1)),
        jnp.int32(0),
    )
    frame_raw = sent_and_summed(row_raw, GY, 0)
    atom_part = sent_and_summed(column_sum, GX, 0)
    frame_sum = exists * frame_raw
    loss_sum, frame_count, atom_count = (
        by_axis(jnp.sum(frame_sum), GX_GY),
        by_axis(jnp.sum(exists), GX_GY),
        by_axis(jnp.sum(weight), GX_GY),
    )
    frame_loss = frame_sum / atom_count
    atom_loss = weight * atom_part / frame_count
    total_loss = (loss_sum / (frame_count * atom_count)).reshape(1)
    return (frame_loss, atom_loss, total_loss)


def solution(mesh):
    finer = Mesh(
        mesh.devices.reshape(mesh.shape["sa"], 8, 2, 4, 2), ("sa", "gx_0", "gx_1", "gy_0", "gy_1")
    )
    placed = (
        P(None, SA_GX_GY),
        P(None, SA_GX_GY),
        P(None, SA_GX_GY),
        P(None, SA_GX_GY),
        P(SA_GX_GY),
        P(SA_GX_GY),
        P(SA_GX_GY),
    )
    return jax.shard_map(
        shards,
        mesh=finer,
        in_specs=placed,
        out_specs=(P(SA_GX_GY), P(SA_GX_GY), P("sa")),
        check_vma=False,
    )
```

profile of v0, /device:TPU:1, one launch (start us, length us, event | category | flops | bytes accessed | tf_op | source)
XLA Modules:
  0.0 204.2 jit_solution(11149782708440451952)
XLA Ops:
  0.6 0.7 broadcast_compare_fusion.2
  1.3 0.7 convert_element_type.45
  2.0 0.8 fusion.10
  2.7 1.0 multiply_reduce_fusion.4
  3.8 0.1 reduce_sum.120
  3.9 0.1 reduce_sum.123
  4.1 0.1 reshape.528
  4.3 0.6 multiply_reduce_fusion.5
  5.2 0.1 slice.335
  5.4 0.1 add.336
  5.5 0.1 add.341
  5.6 0.2 copy-done
  5.8 0.1 concatenate.6
  5.9 28.7 %all_gather.6 = f32[22,1024]{1,0:T(8,128)S(1)} all-gather(f32[22,128]{1,0:T(8,128)S(1)} %concatenate.6), channel_id=1, replica_groups=mesh['sa'=2,'gx_0'=8,'gx_1'=2,'gy_0'=4,'gy_1'=2] {'gy_0','gy_1'}, dimensions={1}, use_global_device_ids=true | all-gather | bytes 101376 | tf_op jit(solution)/shard_map/all_gather | solution.py:24
  34.8 0.1 broadcast_in_dim.118
  35.0 0.1 broadcast_in_dim.104
  35.1 0.3 copy-done.7
  35.5 0.1 broadcast_in_dim.120
  35.9 0.1 multiply_reduce_fusion.3
  36.1 0.1 reduce_sum.122
  36.3 0.1 reshape.538
  36.4 0.1 copy.36
  36.6 0.1 reshape.532
  36.7 9.4 %gather_fusion = f32[672]{0:T(1024)S(1)} fusion(f32[3,16,14]{2,1,0:T(8,128)S(1)} %reshape.529, s32[672]{0:T(1024)S(1)} %reshape.532), kind=kCustom, calls=%fused_computation | custom fusion | bytes 13440 | tf_op jit(solution)/shard_map/jit(take_along_axis)/gather | solution.py:130
  46.1 1.9 gather_fusion.1
  48.1 27.2 %all-gather = f32[16,224,7]{1,2,0:T(8,128)S(1)} all-gather(f32[1,224,7]{1,2,0:T(8,128)S(1)} %maximum_bitcast_fusion), channel_id=1, replica_groups=mesh['sa'=2,'gx_0'=8,'gx_1'=2,'gy_0'=4,'gy_1'=2] {'gx_0','gx_1'}, dimensions={0}, use_global_device_ids=true | all-gather | bytes 106624 | tf_op jit(solution)/shard_map/all_gather | solution.py:31
  75.4 0.1 reshape.548
  75.6 70.5 %while.16 = (s32[]{:T(128)}, f32[1024]{0:T(1024)}, f32[3584]{0:T(1024)S(1)}, f32[3,1024]{1,0:T(4,128)S(1)}, f32[9,1024]{1,0:T(8,128)S(1)}, /*index=5*/f32[3,3584...) while((s32[]{:T(128)}, f32[1024]{0:T(1024)}, ...), condition=%wide.region_7.8_spmd.clone, body=%wide.region_4.7_spmd.clone.sunk | while | flops 82577416 | bytes 480513 | solution.py:183
  75.6 0.1 dynamic-slice_reduce_fusion.7
  75.8 8.3 %multiply_reduce_fusion.15 = f32[896]{0:T(1024)S(1)} fusion(f32[1024]{0:T(1024)S(1)} %bitcast.147, f32[1024]{0:T(1024)S(1)} %bitcast.125, f32[1024]{0:T(1024)S(1)} %bitcast.107, f32[1024]{0:T(1024)S(1)} %bitcast.127, f32[1024]{0:T(1024)S(1)} %bitcast.109, f32[1024]{0:T(1024)S(1)} %bitcast.129, f32[1024]{0:T(1024)S(1)} %bitcast.111, ...), kind=kLoop, calls=%fused_computation.2.clone.1 | loop fusion | flops 41286784 | bytes 115200 | tf_op jit(solution)/shard_map/while/body/eval_jaxpr/reduce_sum | solution.py:179
  84.1 7.8 %multiply_reduce_fusion.14 = f32[1024]{0:T(1024)S(1)} fusion(f32[896]{0:T(1024)S(1)} %multiply_reduce_fusion.13, f32[1024]{0:T(1024)S(1)} %bitcast.126, f32[1024]{0:T(1024)S(1)} %bitcast.108, f32[1024]{0:T(1024)S(1)} %bitcast.128, f32[1024]{0:T(1024)S(1)} %bitcast.110, f32[1024]{0:T(1024)S(1)} %bitcast.130, f32[1024]{0:T(1024)S(1)} %bitcast.112, ...), kind=kLoop, calls=%fused_computation.3.clone.1 | loop fusion | flops 41286656 | bytes 115200 | tf_op jit(solution)/shard_map/while/body/eval_jaxpr/reduce_sum | solution.py:178
  92.0 0.6 select_add_fusion.2
  92.6 0.2 dynamic_update_slice.9
  92.7 0.1 dynamic-slice_reduce_fusion.7
  93.0 8.3 %multiply_reduce_fusion.15 = f32[896]{0:T(1024)S(1)} fusion(f32[1024]{0:T(1024)S(1)} %bitcast.147, f32[1024]{0:T(1024)S(1)} %bitcast.125, f32[1024]{0:T(1024)S(1)} %bitcast.107, f32[1024]{0:T(1024)S(1)} %bitcast.127, f32[1024]{0:T(1024)S(1)} %bitcast.109, f32[1024]{0:T(1024)S(1)} %bitcast.129, f32[1024]{0:T(1024)S(1)} %bitcast.111, ...), kind=kLoop, calls=%fused_computation.2.clone.1 | loop fusion | flops 41286784 | bytes 115200 | tf_op jit(solution)/shard_map/while/body/eval_jaxpr/reduce_sum | solution.py:179
  101.2 7.8 %multiply_reduce_fusion.14 = f32[1024]{0:T(1024)S(1)} fusion(f32[896]{0:T(1024)S(1)} %multiply_reduce_fusion.13, f32[1024]{0:T(1024)S(1)} %bitcast.126, f32[1024]{0:T(1024)S(1)} %bitcast.108, f32[1024]{0:T(1024)S(1)} %bitcast.128, f32[1024]{0:T(1024)S(1)} %bitcast.110, f32[1024]{0:T(1024)S(1)} %bitcast.130, f32[1024]{0:T(1024)S(1)} %bitcast.112, ...), kind=kLoop, calls=%fused_computation.3.clone.1 | loop fusion | flops 41286656 | bytes 115200 | tf_op jit(solution)/shard_map/while/body/eval_jaxpr/reduce_sum | solution.py:178
  109.1 1.3 select_add_fusion.2
  110.3 0.2 dynamic_update_slice.9
  110.5 0.1 dynamic-slice_reduce_fusion.7
  110.7 8.3 %multiply_reduce_fusion.15 = f32[896]{0:T(1024)S(1)} fusion(f32[1024]{0:T(1024)S(1)} %bitcast.147, f32[1024]{0:T(1024)S(1)} %bitcast.125, f32[1024]{0:T(1024)S(1)} %bitcast.107, f32[1024]{0:T(1024)S(1)} %bitcast.127, f32[1024]{0:T(1024)S(1)} %bitcast.109, f32[1024]{0:T(1024)S(1)} %bitcast.129, f32[1024]{0:T(1024)S(1)} %bitcast.111, ...), kind=kLoop, calls=%fused_computation.2.clone.1 | loop fusion | flops 41286784 | bytes 115200 | tf_op jit(solution)/shard_map/while/body/eval_jaxpr/reduce_sum | solution.py:179
  119.0 7.8 %multiply_reduce_fusion.14 = f32[1024]{0:T(1024)S(1)} fusion(f32[896]{0:T(1024)S(1)} %multiply_reduce_fusion.13, f32[1024]{0:T(1024)S(1)} %bitcast.126, f32[1024]{0:T(1024)S(1)} %bitcast.108, f32[1024]{0:T(1024)S(1)} %bitcast.128, f32[1024]{0:T(1024)S(1)} %bitcast.110, f32[1024]{0:T(1024)S(1)} %bitcast.130, f32[1024]{0:T(1024)S(1)} %bitcast.112, ...), kind=kLoop, calls=%fused_computation.3.clone.1 | loop fusion | flops 41286656 | bytes 115200 | tf_op jit(solution)/shard_map/while/body/eval_jaxpr/reduce_sum | solution.py:178
  126.8 1.3 select_add_fusion.2
  128.1 0.2 dynamic_update_slice.9
  128.3 0.1 dynamic-slice_reduce_fusion.7
  128.5 8.3 %multiply_reduce_fusion.15 = f32[896]{0:T(1024)S(1)} fusion(f32[1024]{0:T(1024)S(1)} %bitcast.147, f32[1024]{0:T(1024)S(1)} %bitcast.125, f32[1024]{0:T(1024)S(1)} %bitcast.107, f32[1024]{0:T(1024)S(1)} %bitcast.127, f32[1024]{0:T(1024)S(1)} %bitcast.109, f32[1024]{0:T(1024)S(1)} %bitcast.129, f32[1024]{0:T(1024)S(1)} %bitcast.111, ...), kind=kLoop, calls=%fused_computation.2.clone.1 | loop fusion | flops 41286784 | bytes 115200 | tf_op jit(solution)/shard_map/while/body/eval_jaxpr/reduce_sum | solution.py:179
  136.8 7.8 %multiply_reduce_fusion.14 = f32[1024]{0:T(1024)S(1)} fusion(f32[896]{0:T(1024)S(1)} %multiply_reduce_fusion.13, f32[1024]{0:T(1024)S(1)} %bitcast.126, f32[1024]{0:T(1024)S(1)} %bitcast.108, f32[1024]{0:T(1024)S(1)} %bitcast.128, f32[1024]{0:T(1024)S(1)} %bitcast.110, f32[1024]{0:T(1024)S(1)} %bitcast.130, f32[1024]{0:T(1024)S(1)} %bitcast.112, ...), kind=kLoop, calls=%fused_computation.3.clone.1 | loop fusion | flops 41286656 | bytes 115200 | tf_op jit(solution)/shard_map/while/body/eval_jaxpr/reduce_sum | solution.py:178
  144.6 1.3 select_add_fusion.2
  145.9 0.2 dynamic_update_slice.9
  146.1 6.3 %all-to-all-start = ((f32[8,1,128]{2,1,0:T(1,128)}), f32[8,1,128]{2,1,0:T(1,128)S(1)}, u32[]{:S(2)}, u32[]{:S(2)}) async-start(f32[8,1,128]{2,1,0:T(1,128)} %bitcast.8), calls=%async_computation | async-start | bytes 8192 | tf_op jit(solution)/shard_map/all_to_all | solution.py:47
  152.4 0.1 copy.45
  152.5 0.6 multiply_reduce_fusion.8
  153.1 0.1 broadcast_in_dim.125
  153.2 0.1 reduce_sum.127
  153.3 0.1 reshape.527
  153.5 0.7 all_to_all.14
  154.2 4.5 %all-to-all-done = f32[8,1,128]{2,1,0:T(1,128)S(1)} async-done(((f32[8,1,128]{2,1,0:T(1,128)}), f32[8,1,128]{2,1,0:T(1,128)S(1)}, u32[]{:S(2)}, u32[]{:S(2)}) %all-to-all-start) | async-done | bytes 4128 | tf_op jit(solution)/shard_map/all_to_all | solution.py:47
  158.7 5.4 %all-to-all-start.1 = ((f32[16,1,224]{2,1,0:T(1,128)}), f32[16,1,224]{2,1,0:T(1,128)S(1)}, u32[]{:S(2)}, u32[]{:S(2)}) async-start(f32[16,1,224]{2,1,0:T(1,128)} %all_to_all.14), calls=%async_computation.1 | async-start | bytes 32768 | tf_op jit(solution)/shard_map/all_to_all | solution.py:47
  164.1 0.6 multiply_reduce_fusion.9
  164.7 13.9 %all-reduce = (f32[]{:T(128)}, f32[]{:T(128)}, f32[]{:T(128)}) all-reduce(f32[]{:T(128)} %multiply_reduce_fusion.8, f32[]{:T(128)} %get-tuple-element.214, f32[]{:T(128)} %multiply_reduce_fusion.9), channel_id=1, replica_groups=mesh['sa'=2,'gx_0'=8,'gx_1'=2,'gy_0'=4,'gy_1'=2] {'gx_0'}, use_global_device_ids=true, to_apply=%region_10.11 | all-reduce | flops 3 | bytes 24 | tf_op jit(solution)/shard_map/psum | solution.py:52
  178.6 6.9 %all-reduce.3 = (f32[]{:T(128)}, f32[]{:T(128)}, f32[]{:T(128)}) all-reduce(f32[]{:T(128)} %get-tuple-element.237, f32[]{:T(128)} %get-tuple-element.238, f32[]{:T(128)} %get-tuple-element.239), channel_id=1, replica_groups=mesh['sa'=2,'gx_0'=8,'gx_1'=2,'gy_0'=4,'gy_1'=2] {'gx_1'}, use_global_device_ids=true, to_apply=%region_11.12 | all-reduce | flops 3 | bytes 24 | tf_op jit(solution)/shard_map/psum | solution.py:52
  185.5 7.5 %all-reduce.1 = (f32[]{:T(128)}, f32[]{:T(128)}, f32[]{:T(128)}) all-reduce(f32[]{:T(128)} %get-tuple-element.246, f32[]{:T(128)} %get-tuple-element.247, f32[]{:T(128)} %get-tuple-element.248), channel_id=1, replica_groups=mesh['sa'=2,'gx_0'=8,'gx_1'=2,'gy_0'=4,'gy_1'=2] {'gy_0'}, use_global_device_ids=true, to_apply=%region_12.13 | all-reduce | flops 3 | bytes 24 | tf_op jit(solution)/shard_map/psum | solution.py:52
  193.0 5.9 %all-reduce.2 = (f32[]{:T(128)}, f32[]{:T(128)}, f32[]{:T(128)}) all-reduce(f32[]{:T(128)} %get-tuple-element.240, f32[]{:T(128)} %get-tuple-element.241, f32[]{:T(128)} %get-tuple-element.242), channel_id=1, replica_groups=mesh['sa'=2,'gx_0'=8,'gx_1'=2,'gy_0'=4,'gy_1'=2] {'gy_1'}, use_global_device_ids=true, to_apply=%region_13.14 | all-reduce | flops 3 | bytes 24 | tf_op jit(solution)/shard_map/psum | solution.py:52
  198.9 1.2 broadcast_divide_fusion
  202.0 1.1 fusion.16
  (74 shorter events, 2.1 us)
Async XLA Ops:
  0.6 3.5 %copy-start.2 = (f32[12,128]{1,0:T(8,128)S(1)}, f32[12,128]{1,0:T(8,128)}, u32[]{:S(2)}) copy-start(f32[12,128]{1,0:T(8,128)} %param.15) | copy-start | bytes 18436
  2.0 2.3 %copy-start.5 = (f32[20,8]{0,1:T(8,128)S(1)}, f32[20,8]{0,1:T(8,128)}, u32[]{:S(2)}) copy-start(f32[20,8]{0,1:T(8,128)} %constant.99.clone) | copy-start | bytes 1924
  2.0 2.3 %copy-start.6 = (f32[20,8]{0,1:T(8,128)S(1)}, f32[20,8]{0,1:T(8,128)}, u32[]{:S(2)}) copy-start(f32[20,8]{0,1:T(8,128)} %constant.98.clone) | copy-start | bytes 1924
  3.7 1.2 copy-start.8
  5.1 0.7 copy-start
  34.7 0.7 copy-start.7
  34.7 1.1 copy-start.3
  34.7 1.2 copy-start.1
  46.1 2.0 copy-start.4
  146.1 12.7 %all-to-all-start = ((f32[8,1,128]{2,1,0:T(1,128)}), f32[8,1,128]{2,1,0:T(1,128)S(1)}, u32[]{:S(2)}, u32[]{:S(2)}) async-start(f32[8,1,128]{2,1,0:T(1,128)} %bitcast.8), calls=%async_computation | async-start | bytes 8192 | tf_op jit(solution)/shard_map/all_to_all | solution.py:47
  158.7 43.2 %all-to-all-start.1 = ((f32[16,1,224]{2,1,0:T(1,128)}), f32[16,1,224]{2,1,0:T(1,128)S(1)}, u32[]{:S(2)}, u32[]{:S(2)}) async-start(f32[16,1,224]{2,1,0:T(1,128)} %all_to_all.14), calls=%async_computation.1 | async-start | bytes 32768 | tf_op jit(solution)/shard_map/all_to_all | solution.py:47
where the time goes:
time: 206 us; the launch traced here: 204 us
  blocking collectives  90.1 us (44%)
  other arithmetic  76.6 us (37%)
  local copies, waits for them, and re-layouts  17.1 us (8%)
  starting transfers between devices  11.7 us (6%)
  waiting for transfers between devices  4.53 us (2%)
  between operations  4.01 us (2%)
    psum x4, blocking collectives, by_axis(): return functools.reduce(lax.psum, axes, value)  34.1 us
    reduce_sum x4, other arithmetic, one_block(): column_sums = jnp.sum(clamped * row_exists[:, None], axis=0)  33 us
    reduce_sum x4, other arithmetic, one_block(): frame_raw = frame_raw + jnp.sum(clamped * weight_block, axis=1)  31.3 us
    all_gather x1, blocking collectives, side_by_side(): result = lax.all_gather(both, axis, axis=dim, tiled=True)  28.7 us
    all_gather x1, blocking collectives, gather_turned(): lax.all_gather(both, axis, axis=0, tiled=True)  27.2 us
    all_to_all x2, starting transfers between devices, sent_and_summed(): lax.all_to_all(tiles, axis, split_axis=0, concat_axis=0, tiled=True)  11.7 us
    gather x3, local copies, waits for them, and re-layouts, atom_terms(): jnp.take_along_axis(shaped, jnp.broadcast_to(source[None], shaped.shape),...  9.56 us
    all_to_all x2, waiting for transfers between devices, sent_and_summed(): lax.all_to_all(tiles, axis, split_axis=0, concat_axis=0, tiled=True)  4.53 us
  transfers between devices with their start and end apart: 2, of which 1 were waited for; matrix products, arithmetic and copies ran while one was open for 1% of the time, Pallas kernels for 0%

commit v1 on v0

v1 whole, which is shorter than its diff:
```python
import functools

import jax
import jax.numpy as jnp
import numpy as np
from jax import lax
from jax.experimental import pallas as pl
from jax.experimental.pallas import tpu as pltpu
from jax.sharding import PartitionSpec as P

F32 = jnp.float32
BF16 = jnp.bfloat16
MESH = pl.DeviceIdType.MESH

RESIDUES = 16
FRAMES = 8 * RESIDUES
ATOMS = 14 * RESIDUES
KEPT = 6 * RESIDUES
COLS = 256
FB = 32
DEPTH = 32
EPS = 1e-6
ATOM_COUNTS = (5, 11, 8, 8, 6, 9, 9, 4, 10, 8, 8, 9, 8, 11, 7, 6, 7, 14, 12, 7)
CHI_COUNTS = (0, 4, 2, 2, 1, 3, 3, 0, 2, 2, 2, 4, 3, 2, 2, 1, 1, 2, 2, 1)


def tables():
    lane = np.arange(COLS)
    spread_atoms = (np.arange(128)[:, None] == lane[None] // 14) & (lane[None] < ATOMS)
    spread_frames = np.arange(128)[:, None] == np.arange(FRAMES)[None] // 8
    kept = np.arange(KEPT)
    slot = np.where(kept % 6 == 0, 0, kept % 6 + 2)
    keep = (8 * (kept // 6) + slot)[:, None] == np.arange(FRAMES)[None]
    frame_pick = np.zeros((48, 3 * 128), np.float32)
    atom_pick = np.zeros((DEPTH, 24), np.float32)
    for c in range(3):
        k = 0
        for i in range(3):
            for cc in range(3):
                if cc == c:
                    frame_pick[12, c * 128 + k] = 1.0
                atom_pick[k, 8 * i + cc] = 1.0
                k += 1
        for j, i in ((0, 0), (0, 1), (0, 2), (1, 0), (1, 1), (2, 0)):
            for b in range(3):
                frame_pick[16 * j + 3 * c + b, c * 128 + k] = 1.0
                atom_pick[k, 8 * i + 3 + b] = 1.0
                k += 1
        for j in range(3):
            frame_pick[16 * j + 9 + c, c * 128 + k] = 1.0
            atom_pick[k, 6] = 1.0
            k += 1
    return tuple(
        jnp.asarray(np.asarray(t, np.float32), BF16)
        for t in (spread_atoms, spread_frames, keep, frame_pick, atom_pick)
    )


def dot(a, b):
    return jnp.dot(a, b, preferred_element_type=F32)


def dot_nt(a, b):
    return lax.dot_general(a, b, (((1,), (1,)), ((), ())), preferred_element_type=F32)


def pieces(x, count):
    parts = []
    for _ in range(count):
        part = x.astype(BF16).astype(F32)
        parts.append(part)
        x = x - part
    return parts


def by_type(types, values):
    total = jnp.zeros(types.shape, F32)
    for k, value in enumerate(values):
        total = jnp.where(types == k, F32(value), total)
    return total


def kernel(
    nx, ny,
    pf_hbm, tf_hbm, pa_hbm, ta_hbm, mask_hbm, type_hbm, swap_hbm,
    sa_hbm, sf_hbm, keep_hbm, fpick_hbm, apick_hbm,
    floss_ref, aloss_ref, total_ref,
    pf, tf, pa, ta, mask, types, swaps, spread_a, spread_f, keep, fpick, apick,
    res, frames, atoms, lhs, rhs, acc_f,
    asend, arecv, fsums, totals,
    in_sem, fs_sem, fr_sem, as_sem, ar_sem, ps_sem, pr_sem, ss_sem, sr_sem, ts_sem, tr_sem,
):
    gx, gy = lax.axis_index("gx"), lax.axis_index("gy")

    def at_x(r):
        return {"gx": lax.rem(gx + r, nx)}

    def at_y(r):
        return {"gy": lax.rem(gy + r, ny)}

    barrier = pltpu.get_barrier_semaphore()
    for r in range(1, nx):
        pl.semaphore_signal(barrier, inc=1, device_id=at_x(r), device_id_type=MESH)
    for r in range(1, ny):
        pl.semaphore_signal(barrier, inc=1, device_id=at_y(r), device_id_type=MESH)

    loads = [
        pltpu.make_async_copy(src, dst, in_sem.at[k])
        for k, (src, dst) in enumerate(
            (
                (type_hbm, types), (swap_hbm, swaps), (sa_hbm, spread_a), (sf_hbm, spread_f),
                (pf_hbm, pf), (tf_hbm, tf), (pa_hbm, pa), (ta_hbm, ta), (mask_hbm, mask),
                (keep_hbm, keep), (fpick_hbm, fpick), (apick_hbm, apick),
            )
        )
    ]
    for load in loads:
        load.start()
    res[...] = jnp.zeros_like(res)
    atoms[0] = jnp.zeros((8, COLS), F32)
    acc_f[...] = jnp.zeros_like(acc_f)
    for load in loads:
        load.wait()

    kind, swap = types[...], swaps[...] == 1
    first = (kind == 3) | (kind == 13) | (kind == 18)
    third = (kind == 13) | (kind == 18)
    res[0:1, 0:RESIDUES] = by_type(kind, ATOM_COUNTS)
    res[1:2, 0:RESIDUES] = by_type(kind, CHI_COUNTS)
    res[2:3, 0:RESIDUES] = jnp.where(first & swap, F32(1), F32(0))
    res[3:4, 0:RESIDUES] = jnp.where((kind == 6) & swap, F32(1), F32(0))
    res[4:5, 0:RESIDUES] = jnp.where(third & swap, F32(1), F32(0))
    table = res[...].astype(BF16)
    of_atom = dot(table, spread_a[...])
    of_frame = dot(table, spread_f[...])

    lane = lax.broadcasted_iota(jnp.int32, (1, COLS), 1)
    slot = lane - 14 * ((lane * 4682) >> 16)
    swap_a, swap_b, swap_c = (of_atom[k : k + 1] > 0.5 for k in (2, 3, 4))
    upper = ((slot == 6) & swap_a) | ((slot == 7) & swap_b) | ((slot == 8) & swap_c)
    lower = ((slot == 7) & swap_a) | ((slot == 8) & swap_b) | ((slot == 9) & swap_c)
    atoms[0, 0:3, 0:ATOMS] = pa[...]
    atoms[0, 3:6, 0:ATOMS] = ta[...]
    atoms[0, 6:7, 0:ATOMS] = mask[...].astype(F32)
    raw = atoms[0]
    row = lax.broadcasted_iota(jnp.int32, (8, COLS), 0)
    renamed = jnp.where(
        upper & (row >= 3), pltpu.roll(raw, COLS - 1, 1),
        jnp.where(lower & (row >= 3), pltpu.roll(raw, 1, 1), raw),
    )
    weight = jnp.where(slot.astype(F32) < of_atom[0:1], renamed[6:7], F32(0))
    atoms[0] = renamed * jnp.where(row < 3, F32(0.1), F32(1.0)) * weight

    group = lax.broadcasted_iota(jnp.int32, (1, FRAMES), 1) & 7
    exists = jnp.where(
        (group == 0) | (group == 3) | ((group >= 4) & ((group - 3).astype(F32) <= of_frame[1:2])),
        F32(1), F32(0),
    )
    flips = ((group == 5) & (of_frame[2:3] > 0.5)) | ((group == 6) & (of_frame[3:4] > 0.5))
    sign = jnp.where(flips, F32(-1), F32(1))
    rot_p = [pf[k : k + 1] for k in range(12)]
    rot_t = [tf[k : k + 1] * sign if k % 3 and k < 9 else tf[k : k + 1] for k in range(12)]
    scale = -0.1 * exists
    for a in range(3):
        moved = rot_p[9 + a] * scale
        for b in range(3):
            turn = scale * (
                rot_p[3 * a] * rot_t[3 * b]
                + rot_p[3 * a + 1] * rot_t[3 * b + 1]
                + rot_p[3 * a + 2] * rot_t[3 * b + 2]
            )
            frames[0, 3 * a + b : 3 * a + b + 1] = turn
            moved = moved - turn * rot_t[9 + b]
        frames[0, 9 + a : 10 + a] = moved
    frames[0, 12:13] = exists
    frames[0, 13:16] = jnp.zeros((3, FRAMES), F32)

    pl.semaphore_wait(barrier, nx - 1 + ny - 1)

    def frame_copy(r):
        return pltpu.make_async_remote_copy(
            frames.at[0], frames.at[r], fs_sem.at[r], fr_sem.at[r], at_y(r), MESH
        )

    def atom_copy(r):
        return pltpu.make_async_remote_copy(
            atoms.at[0], atoms.at[r], as_sem.at[r], ar_sem.at[r], at_x(r), MESH
        )

    for r in range(1, nx):
        atom_copy(r).start()
    for r in range(1, ny):
        frame_copy(r).start()

    for s in range(ny):
        if s:
            frame_copy(s).wait_recv()
        split = jnp.concatenate(pieces(frames[s], 3), axis=0).astype(BF16)
        turned = dot_nt(keep[...], split).astype(BF16)
        side = dot(turned, fpick[...]).astype(BF16)
        for q in range(KEPT // FB):
            for c in range(3):
                lhs[s * (KEPT // FB) + q, c * FB : (c + 1) * FB] = side[
                    q * FB : (q + 1) * FB, c * 128 : c * 128 + DEPTH
                ]
    for s in range(nx):
        if s:
            atom_copy(s).wait_recv()
        split = jnp.concatenate(pieces(atoms[s], 3), axis=0).astype(BF16)
        rhs[s] = dot(apick[...], split).astype(BF16)

    def sum_copy(s):
        return pltpu.make_async_remote_copy(
            asend.at[s], arecv.at[s], ss_sem.at[s], sr_sem.at[s], at_x(nx - s), MESH
        )

    def segment(s, carry):
        block = rhs[s]
        columns = jnp.zeros((8, COLS), F32)
        for q in range(ny * KEPT // FB):
            e = dot(lhs[q], block)
            e0, e1, e2 = e[:FB], e[FB : 2 * FB], e[2 * FB :]
            y = jnp.minimum((e0 * e0 + e1 * e1) + (e2 * e2 + EPS), 1.0)
            clamped = y * lax.rsqrt(y)
            acc_f[q * FB : (q + 1) * FB] += clamped[:, :128] + clamped[:, 128:]
            columns = columns + clamped.reshape(FB // 8, 8, COLS).sum(axis=0)
        asend[s] = columns.sum(axis=0, keepdims=True)

        @pl.when(s > 0)
        def _():
            sum_copy(s).start()

        return carry

    lax.fori_loop(0, nx, segment, 0)

    row8 = lax.broadcasted_iota(jnp.int32, (8, 128), 0)
    partial = jnp.zeros((8, KEPT), F32)
    for s in range(ny):
        ones = jnp.where(row8 == s, F32(1), F32(0)).astype(BF16)
        for part in pieces(acc_f[s * KEPT : (s + 1) * KEPT], 3):
            partial = partial + dot_nt(ones, part.astype(BF16))
    wsum = jnp.zeros((1, COLS), F32)
    for s in range(nx):
        wsum = wsum + atoms[s, 6:7]
    fsums[0, 0:8, :] = jnp.zeros((8, 128), F32)
    fsums[0, 0:8, 0:KEPT] = partial
    fsums[0, 8:16, :] = jnp.broadcast_to(wsum[:, :128] + wsum[:, 128:], (8, 128))

    def part_copy(r):
        return pltpu.make_async_remote_copy(
            fsums.at[0], fsums.at[r], ps_sem.at[r], pr_sem.at[r], at_y(r), MESH
        )

    for r in range(1, ny):
        part_copy(r).start()
    fcount = jnp.zeros((1, FRAMES), F32)
    for s in range(ny):
        fcount = fcount + frames[s, 12:13]
    for r in range(1, ny):
        part_copy(r).wait_recv()
    both = fsums[0]
    own = fsums[0, 0:1]
    for r in range(1, ny):
        both = both + fsums[r]
        own = own + fsums[r, ny - r : ny - r + 1]
    atom_count = jnp.sum(both[8:9], axis=1, keepdims=True)
    totals[0, 0:1] = jnp.sum(both[0:8], axis=0, keepdims=True)
    totals[0, 1:8] = jnp.broadcast_to(fcount, (7, 128))

    def total_copy(r):
        return pltpu.make_async_remote_copy(
            totals.at[0], totals.at[r], ts_sem.at[r], tr_sem.at[r], at_x(r), MESH
        )

    for r in range(1, nx):
        total_copy(r).start()

    least_y = jnp.zeros((1, 128), F32) * own + EPS
    least = least_y * lax.rsqrt(least_y)
    columns = F32(nx * ny * COLS)
    rows = F32(nx * ny * KEPT)
    own_sum = jnp.zeros((1, FRAMES), F32)
    for part in pieces(own[:, :KEPT], 3):
        own_sum = own_sum + dot(part.astype(BF16), keep[...])
    floss_ref[...] = (
        frames[0, 12:13] * (own_sum - (columns - atom_count) * least) / atom_count
    )
    for s in range(1, nx):
        sum_copy(s).wait_recv()
    asum = asend[0]
    for s in range(1, nx):
        asum = asum + arecv[s]

    for r in range(1, nx):
        total_copy(r).wait_recv()
    both = totals[0]
    for r in range(1, nx):
        both = both + totals[r]
    frame_count = jnp.sum(both[1:2], axis=1, keepdims=True)
    numerator = jnp.sum(both[0:1], axis=1, keepdims=True)
    pairs = frame_count * atom_count
    total_ref[...] = (numerator - least * (rows * columns - pairs)) / pairs
    wide = jnp.concatenate([least, least], axis=1)
    aloss_ref[...] = (atoms[0, 6:7] * (asum - (rows - frame_count) * wide) / frame_count)[:, :ATOMS]

    for r in range(1, nx):
        atom_copy(r).wait_send()
        sum_copy(r).wait_send()
        total_copy(r).wait_send()
    for r in range(1, ny):
        frame_copy(r).wait_send()
        part_copy(r).wait_send()


def shards(nx, ny, pred_frames, true_frames, pred_atoms, true_atoms, atom_mask, residue_types, swap_flags):
    consts = tables()
    dma = pltpu.SemaphoreType.DMA
    blocks = ny * KEPT // FB
    ins = (
        pred_frames, true_frames, pred_atoms, true_atoms, atom_mask.reshape(1, ATOMS),
        residue_types.reshape(1, RESIDUES), swap_flags.reshape(1, RESIDUES), *consts,
    )
    floss, aloss, total = pl.pallas_call(
        functools.partial(kernel, nx, ny),
        out_shape=(
            jax.ShapeDtypeStruct((1, FRAMES), F32),
            jax.ShapeDtypeStruct((1, ATOMS), F32),
            jax.ShapeDtypeStruct((1, 128), F32),
        ),
        in_specs=[pl.BlockSpec(memory_space=pl.ANY)] * len(ins),
        out_specs=(pl.BlockSpec(memory_space=pltpu.VMEM),) * 3,
        scratch_shapes=[pltpu.VMEM(a.shape, a.dtype) for a in ins]
        + [
            pltpu.VMEM((8, 128), F32),
            pltpu.VMEM((ny, 16, FRAMES), F32),
            pltpu.VMEM((nx, 8, COLS), F32),
            pltpu.VMEM((blocks, 3 * FB, DEPTH), BF16),
            pltpu.VMEM((nx, DEPTH, COLS), BF16),
            pltpu.VMEM((ny * KEPT, 128), F32),
            pltpu.VMEM((nx, 1, COLS), F32),
            pltpu.VMEM((nx, 1, COLS), F32),
            pltpu.VMEM((ny, 16, 128), F32),
            pltpu.VMEM((nx, 8, 128), F32),
            dma((len(ins),)),
            dma((ny,)), dma((ny,)), dma((nx,)), dma((nx,)),
            dma((ny,)), dma((ny,)), dma((nx,)), dma((nx,)), dma((nx,)), dma((nx,)),
        ],
        compiler_params=pltpu.CompilerParams(collective_id=0, has_side_effects=True),
        name="fape",
    )(*ins)
    return floss.reshape(FRAMES), aloss.reshape(ATOMS), total[0, :1]


def solution(mesh):
    whole = ("sa", "gx", "gy")
    wide, flat = P(None, whole), P(whole)
    return jax.shard_map(
        functools.partial(shards, mesh.shape["gx"], mesh.shape["gy"]),
        mesh=mesh,
        in_specs=(wide, wide, wide, wide, flat, flat, flat),
        out_specs=(flat, flat, P("sa")),
        check_vma=False,
    )
```

time: 206 us -> 42.6 us (0.21)
  blocking collectives: 90.1 us -> 0 us
  other arithmetic: 76.6 us -> 0 us
  Pallas kernels: 0 us -> 38.8 us
  local copies, waits for them, and re-layouts: 17.1 us -> 1.83 us
  starting transfers between devices: 11.7 us -> 0 us
  waiting for transfers between devices: 4.53 us -> 0 us
  between operations: 4.01 us -> 1.82 us
    reduce_sum x15 -> x0, other arithmetic: 67.4 us -> none  [the longest x4 33 us: one_block(): column_sums = jnp.sum(clamped * row_exists[:, None], axis=0)]
    all_gather x2 -> x0, blocking collectives: 55.9 us -> none  [the longest x1 28.7 us: side_by_side(): result = lax.all_gather(both, axis, axis=dim, tiled=True)]
    pallas_call x0 -> x1, Pallas kernels: none -> 38.8 us  [shards(): pl.pallas_call(functools.partial(kernel, nx, ny), out_shape=(jax.ShapeDty...]
    psum x4 -> x0, blocking collectives: 34.1 us -> none  [by_axis(): return functools.reduce(lax.psum, axes, value)]
    gather x8 -> x0, local copies, waits for them, and re-layouts: 11.8 us -> none  [the longest x3 9.56 us: atom_terms(): jnp.take_along_axis(shaped, jnp.broadcast_to(source[None], shaped.shape),...]
    all_to_all x2 -> x0, starting transfers between devices: 11.7 us -> none  [sent_and_summed(): lax.all_to_all(tiles, axis, split_axis=0, concat_axis=0, tiled=True)]
    all_to_all x2 -> x0, waiting for transfers between devices: 4.53 us -> none  [sent_and_summed(): lax.all_to_all(tiles, axis, split_axis=0, concat_axis=0, tiled=True)]
    add x7 -> x0, other arithmetic: 4.43 us -> none  [the longest x4 4.41 us: one_block(): frame_raw = frame_raw + jnp.sum(clamped * weight_block, axis=1)]
  transfers between devices with their start and end apart: 2 -> 0, of which waited for: 1 -> 0; matrix products, arithmetic and copies ran while one was open for 1% -> 0% of each run, Pallas kernels for 0% -> 0%
where the time goes in v1:
time: 42.6 us; the launch traced here: 42.5 us
  Pallas kernels  38.8 us (91%)
  local copies, waits for them, and re-layouts  1.83 us (4%)
  between operations  1.82 us (4%)
    pallas_call x1, Pallas kernels, shards(): pl.pallas_call(functools.partial(kernel, nx, ny), out_shape=(jax.ShapeDty...  38.8 us
    unnamed x8, local copies, waits for them, and re-layouts  1.83 us

profile of v1, /device:TPU:1, one launch (start us, length us, event | category | flops | bytes accessed | tf_op | source)
XLA Modules:
  0.0 42.5 jit_solution(13271298314600728449)
XLA Ops:
  0.6 38.8 %fape.1 = (f32[1,128]{1,0:T(1,128)}, f32[1,224]{1,0:T(1,128)}, f32[1,128]{1,0:T(1,128)}) custom-call(f32[12,128]{1,0:T(8,128)} %pf_hbm.1, f32[12,128]{1,0:T(8,128)} %tf_hbm.1, f32[3,224]{1,0:T(4,128)} %pa_hbm.1, f32[3,224]{1,0:T(4,128)} %ta_hbm.1, s32[1,224]{1,0:T(1,128)} %bitcast.7, s32[1,16]{1,0:T(1,128)} %bitcast.9, s32[1,16]{1,0:T(1,128)} %bitcast.10, ...), custom_call_target="tpu_custom_call" | custom-call | tf_op jit(solution)/shard_map/fape/pallas_call | solution.py:324
  39.4 0.0 copy-start.2
  39.5 0.6 %copy-done.2 = f32[1,128]{1,0:T(1,128)S(1)} copy-done((f32[1,128]{1,0:T(1,128)S(1)}, f32[1,128]{1,0:T(1,128)}, u32[]{:S(2)}) %copy-start.2) | copy-done | bytes 536
  40.1 0.0 copy-start
  40.1 0.5 %copy.18 = f32[128]{0:T(128)} copy(f32[128]{0:T(128)S(1)} %bitcast.12) | data formatting | bytes 1024
  40.6 0.1 copy-done
  40.7 0.0 copy-start.1
  40.7 0.6 %copy.19 = f32[224]{0:T(256)} copy(f32[224]{0:T(256)S(1)} %bitcast.8) | data formatting | bytes 1792
  41.3 0.0 copy-done.1
Async XLA Ops:
  39.4 0.6 %copy-start.2 = (f32[1,128]{1,0:T(1,128)S(1)}, f32[1,128]{1,0:T(1,128)}, u32[]{:S(2)}) copy-start(f32[1,128]{1,0:T(1,128)} %get-tuple-element.6) | copy-start | bytes 1540
  40.1 0.6 %copy-start = (f32[1,224]{1,0:T(1,128)S(1)}, f32[1,224]{1,0:T(1,128)}, u32[]{:S(2)}) copy-start(f32[1,224]{1,0:T(1,128)} %get-tuple-element.7) | copy-start | bytes 2692
  40.7 0.6 %copy-start.1 = (f32[1,128]{1,0:T(1,128)S(1)}, f32[1,128]{1,0:T(1,128)}, u32[]{:S(2)}) copy-start(f32[1,128]{1,0:T(1,128)} %get-tuple-element.8) | copy-start | bytes 1540

commit v2 on v1

v2 whole, which is shorter than its diff:
```python
import functools

import jax
import jax.numpy as jnp
import numpy as np
from jax import lax
from jax.experimental import pallas as pl
from jax.experimental.pallas import tpu as pltpu
from jax.sharding import PartitionSpec as P

F32 = jnp.float32
BF16 = jnp.bfloat16
MESH = pl.DeviceIdType.MESH

RESIDUES = 16
FRAMES = 8 * RESIDUES
ATOMS = 14 * RESIDUES
KEPT = 6 * RESIDUES
COLS = 256
FB = 32
DEPTH = 32
EPS = 1e-6
ATOM_COUNTS = (5, 11, 8, 8, 6, 9, 9, 4, 10, 8, 8, 9, 8, 11, 7, 6, 7, 14, 12, 7)
CHI_COUNTS = (0, 4, 2, 2, 1, 3, 3, 0, 2, 2, 2, 4, 3, 2, 2, 1, 1, 2, 2, 1)


def tables():
    spread = np.zeros((RESIDUES, 384), np.float32)
    for k in range(ATOMS):
        spread[k // 14, k] = 1.0
    for k in range(FRAMES):
        spread[k // 8, COLS + k] = 1.0
    keep = np.zeros((KEPT, 384), np.float32)
    for k in range(KEPT):
        keep[k, 8 * (k // 6) + (k % 6 + 2 if k % 6 else 0)] = 1.0
    frame_pick = np.zeros((48, 384), np.float32)
    atom_pick = np.zeros((DEPTH, 384), np.float32)
    for c in range(3):
        k = 0
        for i in range(3):
            for cc in range(3):
                if cc == c:
                    frame_pick[12, c * 128 + k] = 1.0
                atom_pick[k, 8 * i + cc] = 1.0
                k += 1
        for j, i in ((0, 0), (0, 1), (0, 2), (1, 0), (1, 1), (2, 0)):
            for b in range(3):
                frame_pick[16 * j + 3 * c + b, c * 128 + k] = 1.0
                atom_pick[k, 8 * i + 3 + b] = 1.0
                k += 1
        for j in range(3):
            frame_pick[16 * j + 9 + c, c * 128 + k] = 1.0
            atom_pick[k, 6] = 1.0
            k += 1
    return jnp.asarray(np.concatenate([spread, keep, frame_pick, atom_pick]), BF16)


def dot(a, b):
    return jnp.dot(a, b, preferred_element_type=F32)


def dot_nt(a, b):
    return lax.dot_general(a, b, (((1,), (1,)), ((), ())), preferred_element_type=F32)


def pieces(x, count):
    parts = []
    for _ in range(count):
        part = x.astype(BF16).astype(F32)
        parts.append(part)
        x = x - part
    return parts


def by_type(types, values):
    total = jnp.zeros(types.shape, F32)
    for k, value in enumerate(values):
        total = jnp.where(types == k, F32(value), total)
    return total


def all_of(ref, sem):
    pltpu.make_async_copy(ref, ref, sem).wait()


def kernel(
    nx, ny,
    pf_hbm, tf_hbm, pa_hbm, ta_hbm, mask_hbm, type_hbm, swap_hbm, consts_hbm,
    out_ref,
    pf, tf, pa, ta, mask, types, swaps, consts,
    res, frames, atoms, lhs, rhs, acc_f, acc_c,
    asend, arecv, psend, precv, tsend, usend,
    in_sem, send_sem, frame_sem, atom_sem, sum_sem, part_sem, total_sems,
):
    gx, gy = lax.axis_index("gx"), lax.axis_index("gy")
    nz, nw = nx // 2, ny // 2
    z, core, w, half = lax.div(gx, 2), lax.rem(gx, 2), lax.div(gy, 2), lax.rem(gy, 2)
    near_z = [0] + [d for k in range(1, nz // 2 + 1) for d in sorted({k, nz - k})]
    near_w = [0] + [d for k in range(1, nw // 2 + 1) for d in sorted({k, nw - k})]

    def to_x(j):
        return {"gx": 2 * lax.rem(z + near_z[j // 2], nz) + lax.rem(core + j % 2, 2)}

    def from_x(j):
        return {"gx": 2 * lax.rem(z + nz - near_z[j // 2], nz) + lax.rem(core + j % 2, 2)}

    def to_y(j):
        return {"gy": 2 * lax.rem(w + near_w[j % nw], nw) + lax.rem(half + j // nw, 2)}

    def from_y(j):
        return {"gy": 2 * lax.rem(w + nw - near_w[j % nw], nw) + lax.rem(half + j // nw, 2)}

    barrier = pltpu.get_barrier_semaphore()
    for j in range(1, nx):
        pl.semaphore_signal(barrier, inc=1, device_id=to_x(j), device_id_type=MESH)
    for j in range(1, ny):
        pl.semaphore_signal(barrier, inc=1, device_id=to_y(j), device_id_type=MESH)

    loads = [
        pltpu.make_async_copy(src, dst, in_sem.at[k])
        for k, (src, dst) in enumerate(
            (
                (type_hbm, types), (swap_hbm, swaps), (consts_hbm, consts), (pf_hbm, pf),
                (tf_hbm, tf), (pa_hbm, pa), (ta_hbm, ta), (mask_hbm, mask),
            )
        )
    ]
    for load in loads:
        load.start()
    res[...] = jnp.zeros_like(res)
    atoms[0] = jnp.zeros((8, COLS), F32)
    acc_f[...] = jnp.zeros_like(acc_f)
    for load in loads:
        load.wait()
    spread = consts[0:RESIDUES]
    keep = consts[RESIDUES : RESIDUES + KEPT, 0:128]
    fpick = consts[RESIDUES + KEPT : RESIDUES + KEPT + 48]
    apick = consts[RESIDUES + KEPT + 48 : RESIDUES + KEPT + 48 + DEPTH, 0:24]

    kind, swap = types[...], swaps[...] == 1
    first = (kind == 3) | (kind == 13) | (kind == 18)
    third = (kind == 13) | (kind == 18)
    res[0:1, 0:RESIDUES] = by_type(kind, ATOM_COUNTS)
    res[1:2, 0:RESIDUES] = by_type(kind, CHI_COUNTS)
    res[2:3, 0:RESIDUES] = jnp.where(first & swap, F32(1), F32(0))
    res[3:4, 0:RESIDUES] = jnp.where((kind == 6) & swap, F32(1), F32(0))
    res[4:5, 0:RESIDUES] = jnp.where(third & swap, F32(1), F32(0))
    of_both = dot(res[:, 0:RESIDUES].astype(BF16), spread)
    of_atom, of_frame = of_both[:, :COLS], of_both[:, COLS:]

    lane = lax.broadcasted_iota(jnp.int32, (1, COLS), 1)
    slot = lane - 14 * ((lane * 4682) >> 16)
    swap_a, swap_b, swap_c = (of_atom[k : k + 1] > 0.5 for k in (2, 3, 4))
    upper = ((slot == 6) & swap_a) | ((slot == 7) & swap_b) | ((slot == 8) & swap_c)
    lower = ((slot == 7) & swap_a) | ((slot == 8) & swap_b) | ((slot == 9) & swap_c)
    atoms[0, 0:3, 0:ATOMS] = pa[...]
    atoms[0, 3:6, 0:ATOMS] = ta[...]
    atoms[0, 6:7, 0:ATOMS] = mask[...].astype(F32)
    raw = atoms[0]
    row = lax.broadcasted_iota(jnp.int32, (8, COLS), 0)
    renamed = jnp.where(
        upper & (row >= 3), pltpu.roll(raw, COLS - 1, 1),
        jnp.where(lower & (row >= 3), pltpu.roll(raw, 1, 1), raw),
    )
    weight = jnp.where(slot.astype(F32) < of_atom[0:1], renamed[6:7], F32(0))
    atoms[0] = renamed * jnp.where(row < 3, F32(0.1), F32(1.0)) * weight

    group = lax.broadcasted_iota(jnp.int32, (1, FRAMES), 1) & 7
    exists = jnp.where(
        (group == 0) | (group == 3) | ((group >= 4) & ((group - 3).astype(F32) <= of_frame[1:2])),
        F32(1), F32(0),
    )
    flips = ((group == 5) & (of_frame[2:3] > 0.5)) | ((group == 6) & (of_frame[3:4] > 0.5))
    sign = jnp.where(flips, F32(-1), F32(1))
    rot_p = [pf[k : k + 1] for k in range(12)]
    rot_t = [tf[k : k + 1] * sign if k % 3 and k < 9 else tf[k : k + 1] for k in range(12)]
    scale = -0.1 * exists
    for a in range(3):
        moved = rot_p[9 + a] * scale
        for b in range(3):
            turn = scale * (
                rot_p[3 * a] * rot_t[3 * b]
                + rot_p[3 * a + 1] * rot_t[3 * b + 1]
                + rot_p[3 * a + 2] * rot_t[3 * b + 2]
            )
            frames[0, 3 * a + b : 3 * a + b + 1] = turn
            moved = moved - turn * rot_t[9 + b]
        frames[0, 9 + a : 10 + a] = moved
    frames[0, 12:13] = exists
    frames[0, 13:16] = jnp.zeros((3, FRAMES), F32)

    pl.semaphore_wait(barrier, nx - 1 + ny - 1)

    first_part = 6 if nx >= 16 else 2
    middle = (first_part + nx) // 2
    groups = ((0, first_part), (first_part, middle), (middle, nx))
    group_of = [k for k, (low, high) in enumerate(groups) for _ in range(low, high)]
    for j in range(1, ny):
        pltpu.make_async_remote_copy(
            frames.at[0], frames.at[j], send_sem.at[0], frame_sem.at[j], to_y(j), MESH
        ).start()
    for j in range(1, nx):
        pltpu.make_async_remote_copy(
            atoms.at[0], atoms.at[j], send_sem.at[1], atom_sem.at[group_of[j]], to_x(j), MESH
        ).start()

    chunks = KEPT // FB

    def frame_side(s):
        split = jnp.concatenate(pieces(frames[s], 3), axis=0).astype(BF16)
        turned = dot_nt(keep, split).astype(BF16)
        side = dot(turned, fpick).astype(BF16)
        for q in range(chunks):
            for c in range(3):
                lhs[s * chunks + q, c * FB : (c + 1) * FB] = side[
                    q * FB : (q + 1) * FB, c * 128 : c * 128 + DEPTH
                ]

    def atom_side(j):
        split = jnp.concatenate(pieces(atoms[j], 3), axis=0).astype(BF16)
        rhs[j] = dot(apick, split).astype(BF16)

    def pair_block(start, q, segments, sums):
        total = jnp.zeros((FB, 128), F32)
        for k, j in enumerate(segments):
            e = dot(lhs[q], rhs[j])
            e0, e1, e2 = e[:FB], e[FB : 2 * FB], e[2 * FB :]
            y = jnp.minimum((e0 * e0 + e1 * e1) + (e2 * e2 + EPS), 1.0)
            clamped = y * lax.rsqrt(y)
            side = clamped[:, :128] + clamped[:, 128:]
            total = side if k == 0 else total + side
            sums[k] = sums[k] + clamped.reshape(FB // 8, 8, COLS).sum(axis=0)
        acc_f[pl.ds(start, FB)] += total

    def send_sums(segments):
        for j in segments:
            if j:
                pltpu.make_async_remote_copy(
                    asend.at[j], arecv.at[j], send_sem.at[2], sum_sem.at[0], from_x(j), MESH
                ).start()

    nearest = range(first_part)
    frame_side(0)
    atom_side(0)
    all_of(atoms.at[1:first_part], atom_sem.at[0])
    for j in nearest[1:]:
        atom_side(j)
    for j in nearest:
        acc_c[j] = jnp.zeros((8, COLS), F32)

    def one_frame_segment(s, carry):
        @pl.when(s > 0)
        def _():
            all_of(frames.at[s], frame_sem.at[s])
            frame_side(s)

        sums = [acc_c[j] for j in nearest]
        for q in range(chunks):
            start = pl.multiple_of(s * KEPT + q * FB, FB)
            pair_block(start, s * chunks + q, nearest, sums)
        for j in nearest:
            acc_c[j] = sums[j]
        return carry

    lax.fori_loop(0, ny, one_frame_segment, 0)
    running = jnp.zeros((1, COLS), F32)
    for j in nearest:
        asend[j] = acc_c[j].sum(axis=0, keepdims=True)
        running = running + asend[j]
    send_sums(nearest)

    for k, (low, high) in enumerate(groups[1:]):
        segments = range(low, high)
        all_of(atoms.at[low:high], atom_sem.at[k + 1])
        for j in segments:
            atom_side(j)
        sums = [jnp.zeros((8, COLS), F32) for _ in segments]
        for q in range(ny * chunks):
            pair_block(q * FB, q, segments, sums)
        for j, value in zip(segments, sums):
            asend[j] = value.sum(axis=0, keepdims=True)
            running = running + asend[j]
        send_sums(segments)

    frame_flags = frames[0, 12:13]
    for s in range(1, ny):
        frame_flags = frame_flags + frames[s, 12:13]
    tsend[0, 0:1] = running[:, :128] + running[:, 128:]
    tsend[0, 1:2] = frame_flags
    for j in range(1, nx):
        pltpu.make_async_remote_copy(
            tsend.at[0], tsend.at[j], send_sem.at[3], total_sems.at[0], to_x(j), MESH
        ).start()

    ones = jnp.ones((8, 128), BF16)
    weights = jnp.zeros((1, COLS), F32)
    for j in range(nx):
        weights = weights + atoms[j, 6:7]
    psend[...] = jnp.zeros_like(psend)
    for s in range(ny):
        partial = jnp.zeros((8, KEPT), F32)
        for part in pieces(acc_f[s * KEPT : (s + 1) * KEPT], 3):
            partial = partial + dot_nt(ones, part.astype(BF16))
        psend[s, 0:1, 0:KEPT] = partial[0:1]
        psend[s, 1:2] = weights[:, :128] + weights[:, 128:]
        if s:
            pltpu.make_async_remote_copy(
                psend.at[s], precv.at[s], send_sem.at[4], part_sem.at[0], from_y(s), MESH
            ).start()

    all_of(tsend.at[1:nx], total_sems.at[0])
    both = tsend[0]
    for j in range(1, nx):
        both = both + tsend[j]
    usend[0] = both[0:1]
    for j in range(1, ny):
        pltpu.make_async_remote_copy(
            usend.at[0], usend.at[j], send_sem.at[5], total_sems.at[1], to_y(j), MESH
        ).start()
    frame_count = jnp.sum(both[1:2], axis=1, keepdims=True)

    columns = F32(nx * ny * COLS)
    rows = F32(nx * ny * KEPT)
    all_of(precv.at[1:ny], part_sem.at[0])
    mine = psend[0]
    for s in range(1, ny):
        mine = mine + precv[s]
    atom_count = jnp.sum(mine[1:2], axis=1, keepdims=True)
    least_y = jnp.zeros((1, 128), F32) * mine[0:1] + EPS
    least = least_y * lax.rsqrt(least_y)
    own_sum = jnp.zeros((8, FRAMES), F32)
    for part in pieces(jnp.broadcast_to(mine[0:1, :KEPT], (8, KEPT)), 3):
        own_sum = own_sum + dot(part.astype(BF16), keep)
    out_ref[0:1, 0:FRAMES] = (
        frames[0, 12:13] * (own_sum[0:1] - (columns - atom_count) * least) / atom_count
    )
    all_of(arecv.at[1:nx], sum_sem.at[0])
    asum = asend[0]
    for j in range(1, nx):
        asum = asum + arecv[j]
    wide = jnp.concatenate([least, least], axis=1)
    out_ref[1:2, :] = atoms[0, 6:7] * (asum - (rows - frame_count) * wide) / frame_count
    pairs = frame_count * atom_count

    all_of(usend.at[1:ny], total_sems.at[1])
    both = usend[0]
    for j in range(1, ny):
        both = both + usend[j]
    numerator = jnp.sum(both, axis=1, keepdims=True)
    out_ref[2:3, 0:128] = (numerator - least * (rows * columns - pairs)) / pairs

    all_of(frames.at[1:ny], send_sem.at[0])
    all_of(atoms.at[1:nx], send_sem.at[1])
    all_of(arecv.at[1:nx], send_sem.at[2])
    all_of(tsend.at[1:nx], send_sem.at[3])
    all_of(precv.at[1:ny], send_sem.at[4])
    all_of(usend.at[1:ny], send_sem.at[5])


def shards(nx, ny, pred_frames, true_frames, pred_atoms, true_atoms, atom_mask, residue_types, swap_flags):
    dma = pltpu.SemaphoreType.DMA
    blocks = ny * KEPT // FB
    ins = (
        pred_frames, true_frames, pred_atoms, true_atoms, atom_mask.reshape(1, ATOMS),
        residue_types.reshape(1, RESIDUES), swap_flags.reshape(1, RESIDUES), tables(),
    )
    packed = pl.pallas_call(
        functools.partial(kernel, nx, ny),
        out_shape=pltpu.VMEM((8, COLS), F32),
        in_specs=[pl.BlockSpec(memory_space=pl.ANY)] * len(ins),
        out_specs=pl.BlockSpec(memory_space=pltpu.VMEM),
        scratch_shapes=[pltpu.VMEM(a.shape, a.dtype) for a in ins]
        + [
            pltpu.VMEM((8, 128), F32),
            pltpu.VMEM((ny, 16, FRAMES), F32),
            pltpu.VMEM((nx, 8, COLS), F32),
            pltpu.VMEM((blocks, 3 * FB, DEPTH), BF16),
            pltpu.VMEM((nx, DEPTH, COLS), BF16),
            pltpu.VMEM((ny * KEPT, 128), F32),
            pltpu.VMEM((nx, 8, COLS), F32),
            pltpu.VMEM((nx, 1, COLS), F32),
            pltpu.VMEM((nx, 1, COLS), F32),
            pltpu.VMEM((ny, 2, 128), F32),
            pltpu.VMEM((ny, 2, 128), F32),
            pltpu.VMEM((nx, 2, 128), F32),
            pltpu.VMEM((ny, 1, 128), F32),
            dma((len(ins),)), dma((6,)), dma((ny,)), dma((3,)), dma((1,)), dma((1,)), dma((2,)),
        ],
        compiler_params=pltpu.CompilerParams(collective_id=0, has_side_effects=True),
        name="fape",
    )(*ins)
    return packed[0, :FRAMES], packed[1, :ATOMS], packed[2, :1]


def solution(mesh):
    whole = ("sa", "gx", "gy")
    wide, flat = P(None, whole), P(whole)
    return jax.shard_map(
        functools.partial(shards, mesh.shape["gx"], mesh.shape["gy"]),
        mesh=mesh,
        in_specs=(wide, wide, wide, wide, flat, flat, flat),
        out_specs=(flat, flat, P("sa")),
        check_vma=False,
    )
```

time: 42.6 us -> 34.5 us (0.81)
  Pallas kernels: 38.8 us -> 32.2 us
  between operations: 1.82 us -> 0.64 us
    pallas_call x1, Pallas kernels: 38.8 us -> 32.2 us  [shards(): pl.pallas_call(functools.partial(kernel, nx, ny), out_shape=pltpu.VMEM((8...]
    unnamed x8 -> x0, local copies, waits for them, and re-layouts: 1.83 us -> none
    slice x0 -> x2, local copies, waits for them, and re-layouts: none -> 1.08 us  [shards(): return (packed[0, :FRAMES], packed[1, :ATOMS], packed[2, :1])]
    squeeze x0 -> x1, local copies, waits for them, and re-layouts: none -> 0.51 us  [shards(): return (packed[0, :FRAMES], packed[1, :ATOMS], packed[2, :1])]
where the time goes in v2:
time: 34.5 us; the launch traced here: 34.4 us
  Pallas kernels  32.2 us (93%)
  local copies, waits for them, and re-layouts  1.59 us (5%)
  between operations  0.64 us (2%)
    pallas_call x1, Pallas kernels, shards(): pl.pallas_call(functools.partial(kernel, nx, ny), out_shape=pltpu.VMEM((8...  32.2 us
    slice x2, local copies, waits for them, and re-layouts, shards(): return (packed[0, :FRAMES], packed[1, :ATOMS], packed[2, :1])  1.08 us

profile of v2, /device:TPU:1, one launch (start us, length us, event | category | flops | bytes accessed | tf_op | source)
XLA Modules:
  0.0 34.4 jit_solution(7912642848927935730)
XLA Ops:
  0.6 32.2 %fape.1 = f32[8,256]{1,0:T(8,128)S(1)} custom-call(f32[12,128]{1,0:T(8,128)} %pf_hbm.1, f32[12,128]{1,0:T(8,128)} %tf_hbm.1, f32[3,224]{1,0:T(4,128)} %pa_hbm.1, f32[3,224]{1,0:T(4,128)} %ta_hbm.1, s32[1,224]{1,0:T(1,128)} %bitcast.7, s32[1,16]{1,0:T(1,128)} %bitcast.9, s32[1,16]{1,0:T(1,128)} %bitcast.10, bf16[192,384]{1,0:T(8,128)(2,1)} %constant.2.clone.consts_hbm), custom_call_target="tpu_custom_call" | custom-call | tf_op jit(solution)/shard_map/fape/pallas_call | solution.py:367
  32.8 0.5 %slice.11 = f32[1,1]{1,0:T(1,128)} slice(f32[8,256]{1,0:T(8,128)S(1)} %fape.1), slice={[2:3], [0:1]} | slice | bytes 8 | tf_op jit(solution)/shard_map/slice | solution.py:392
  33.4 0.5 %slice_bitcast_fusion = f32[128]{0:T(128)} fusion(f32[8,256]{1,0:T(8,128)S(1)} %fape.1), kind=kLoop, calls=%fused_computation | loop fusion | bytes 1024 | tf_op jit(solution)/shard_map/squeeze | solution.py:392
  33.9 0.6 %slice.10 = f32[1,224]{1,0:T(1,128)} slice(f32[8,256]{1,0:T(8,128)S(1)} %fape.1), slice={[1:2], [0:224]} | slice | bytes 1792 | tf_op jit(solution)/shard_map/slice | solution.py:392

commit v3 on v2

--- a/solution.py
+++ b/solution.py
@@ -84,16 +84,16 @@
 
 
 def kernel(
-    nx, ny,
+    nx, ny, tiles,
     pf_hbm, tf_hbm, pa_hbm, ta_hbm, mask_hbm, type_hbm, swap_hbm, consts_hbm,
     out_ref,
     pf, tf, pa, ta, mask, types, swaps, consts,
-    res, frames, atoms, lhs, rhs, acc_f, acc_c,
+    res, frames, atoms, lhs, rhs, acc_f, packed, unpacked,
     asend, arecv, psend, precv, tsend, usend,
     in_sem, send_sem, frame_sem, atom_sem, sum_sem, part_sem, total_sems,
 ):
     gx, gy = lax.axis_index("gx"), lax.axis_index("gy")
-    nz, nw = nx // 2, ny // 2
+    nz, nw, part = nx // 2, ny // 2, nx // 2
     z, core, w, half = lax.div(gx, 2), lax.rem(gx, 2), lax.div(gy, 2), lax.rem(gy, 2)
     near_z = [0] + [d for k in range(1, nz // 2 + 1) for d in sorted({k, nz - k})]
     near_w = [0] + [d for k in range(1, nw // 2 + 1) for d in sorted({k, nw - k})]
@@ -110,6 +110,10 @@
     def from_y(j):
         return {"gy": 2 * lax.rem(w + nw - near_w[j % nw], nw) + lax.rem(half + j // nw, 2)}
 
+    for j in range(nx):
+        atoms[j, 7:8] = jnp.zeros((1, COLS), F32)
+    for j in range(ny):
+        frames[j, 13:16] = jnp.zeros((3, FRAMES), F32)
     barrier = pltpu.get_barrier_semaphore()
     for j in range(1, nx):
         pl.semaphore_signal(barrier, inc=1, device_id=to_x(j), device_id_type=MESH)
@@ -130,6 +134,9 @@
     res[...] = jnp.zeros_like(res)
     atoms[0] = jnp.zeros((8, COLS), F32)
     acc_f[...] = jnp.zeros_like(acc_f)
+    asend[...] = jnp.zeros_like(asend)
+    if part * ATOMS != tiles * COLS:
+        packed[...] = jnp.zeros_like(packed)
     for load in loads:
         load.wait()
     spread = consts[0:RESIDUES]
@@ -187,22 +194,24 @@
             moved = moved - turn * rot_t[9 + b]
         frames[0, 9 + a : 10 + a] = moved
     frames[0, 12:13] = exists
-    frames[0, 13:16] = jnp.zeros((3, FRAMES), F32)
 
     pl.semaphore_wait(barrier, nx - 1 + ny - 1)
 
-    first_part = 6 if nx >= 16 else 2
-    middle = (first_part + nx) // 2
-    groups = ((0, first_part), (first_part, middle), (middle, nx))
-    group_of = [k for k, (low, high) in enumerate(groups) for _ in range(low, high)]
+    def send_atoms(j):
+        pltpu.make_async_remote_copy(
+            atoms.at[0, 0:7], atoms.at[j, 0:7], send_sem.at[1], atom_sem.at[j // part],
+            to_x(j), MESH,
+        ).start()
+
+    for j in range(1, part):
+        send_atoms(j)
     for j in range(1, ny):
         pltpu.make_async_remote_copy(
-            frames.at[0], frames.at[j], send_sem.at[0], frame_sem.at[j], to_y(j), MESH
+            frames.at[0, 0:13], frames.at[j, 0:13], send_sem.at[0], frame_sem.at[j],
+            to_y(j), MESH,
         ).start()
-    for j in range(1, nx):
-        pltpu.make_async_remote_copy(
-            atoms.at[0], atoms.at[j], send_sem.at[1], atom_sem.at[group_of[j]], to_x(j), MESH
-        ).start()
+    for j in range(part, nx):
+        send_atoms(j)
 
     chunks = KEPT // FB
 
@@ -216,9 +225,13 @@
                     q * FB : (q + 1) * FB, c * 128 : c * 128 + DEPTH
                 ]
 
-    def atom_side(j):
-        split = jnp.concatenate(pieces(atoms[j], 3), axis=0).astype(BF16)
-        rhs[j] = dot(apick, split).astype(BF16)
+    def atom_side(group):
+        for k in range(part):
+            packed[:, k * ATOMS : (k + 1) * ATOMS] = atoms[group * part + k, :, 0:ATOMS]
+        split = jnp.concatenate(pieces(packed[...], 3), axis=0).astype(BF16)
+        side = dot(apick, split).astype(BF16)
+        for t in range(tiles):
+            rhs[group * tiles + t] = side[:, t * COLS : (t + 1) * COLS]
 
     def pair_block(start, q, segments, sums):
         total = jnp.zeros((FB, 128), F32)
@@ -232,55 +245,45 @@
             sums[k] = sums[k] + clamped.reshape(FB // 8, 8, COLS).sum(axis=0)
         acc_f[pl.ds(start, FB)] += total
 
-    def send_sums(segments):
-        for j in segments:
+    def send_sums(group, sums):
+        total = jnp.zeros((1, COLS), F32)
+        for t, value in enumerate(sums):
+            row = value.sum(axis=0, keepdims=True)
+            unpacked[0:1, t * COLS : (t + 1) * COLS] = row
+            total = total + row
+        for k in range(part):
+            j = group * part + k
+            asend[j, :, 0:ATOMS] = unpacked[0:1, k * ATOMS : (k + 1) * ATOMS]
             if j:
                 pltpu.make_async_remote_copy(
                     asend.at[j], arecv.at[j], send_sem.at[2], sum_sem.at[0], from_x(j), MESH
                 ).start()
-
-    nearest = range(first_part)
+        return total
+
+    def wait_frames(s):
+        all_of(frames.at[s, 0:13], frame_sem.at[s])
+        frame_side(s)
+
+    near = ny // 2 + 1
     frame_side(0)
+    all_of(atoms.at[1:part, 0:7], atom_sem.at[0])
     atom_side(0)
-    all_of(atoms.at[1:first_part], atom_sem.at[0])
-    for j in nearest[1:]:
-        atom_side(j)
-    for j in nearest:
-        acc_c[j] = jnp.zeros((8, COLS), F32)
-
-    def one_frame_segment(s, carry):
-        @pl.when(s > 0)
-        def _():
-            all_of(frames.at[s], frame_sem.at[s])
-            frame_side(s)
-
-        sums = [acc_c[j] for j in nearest]
-        for q in range(chunks):
-            start = pl.multiple_of(s * KEPT + q * FB, FB)
-            pair_block(start, s * chunks + q, nearest, sums)
-        for j in nearest:
-            acc_c[j] = sums[j]
-        return carry
-
-    lax.fori_loop(0, ny, one_frame_segment, 0)
-    running = jnp.zeros((1, COLS), F32)
-    for j in nearest:
-        asend[j] = acc_c[j].sum(axis=0, keepdims=True)
-        running = running + asend[j]
-    send_sums(nearest)
-
-    for k, (low, high) in enumerate(groups[1:]):
-        segments = range(low, high)
-        all_of(atoms.at[low:high], atom_sem.at[k + 1])
-        for j in segments:
-            atom_side(j)
-        sums = [jnp.zeros((8, COLS), F32) for _ in segments]
-        for q in range(ny * chunks):
-            pair_block(q * FB, q, segments, sums)
-        for j, value in zip(segments, sums):
-            asend[j] = value.sum(axis=0, keepdims=True)
-            running = running + asend[j]
-        send_sums(segments)
+    for s in range(1, near):
+        wait_frames(s)
+    sums = [jnp.zeros((8, COLS), F32) for _ in range(tiles)]
+    for q in range(near * chunks):
+        pair_block(q * FB, q, range(tiles), sums)
+    for s in range(near, ny):
+        wait_frames(s)
+    for q in range(near * chunks, ny * chunks):
+        pair_block(q * FB, q, range(tiles), sums)
+    running = send_sums(0, sums)
+    all_of(atoms.at[part:nx, 0:7], atom_sem.at[1])
+    atom_side(1)
+    sums = [jnp.zeros((8, COLS), F32) for _ in range(tiles)]
+    for q in range(ny * chunks):
+        pair_block(q * FB, q, range(tiles, 2 * tiles), sums)
+    running = running + send_sums(1, sums)
 
     frame_flags = frames[0, 12:13]
     for s in range(1, ny):
@@ -319,7 +322,7 @@
         ).start()
     frame_count = jnp.sum(both[1:2], axis=1, keepdims=True)
 
-    columns = F32(nx * ny * COLS)
+    columns = F32(2 * tiles * ny * COLS)
     rows = F32(nx * ny * KEPT)
     all_of(precv.at[1:ny], part_sem.at[0])
     mine = psend[0]
@@ -349,8 +352,8 @@
     numerator = jnp.sum(both, axis=1, keepdims=True)
     out_ref[2:3, 0:128] = (numerator - least * (rows * columns - pairs)) / pairs
 
-    all_of(frames.at[1:ny], send_sem.at[0])
-    all_of(atoms.at[1:nx], send_sem.at[1])
+    all_of(frames.at[1:ny, 0:13], send_sem.at[0])
+    all_of(atoms.at[1:nx, 0:7], send_sem.at[1])
     all_of(arecv.at[1:nx], send_sem.at[2])
     all_of(tsend.at[1:nx], send_sem.at[3])
     all_of(precv.at[1:ny], send_sem.at[4])
@@ -360,12 +363,13 @@
 def shards(nx, ny, pred_frames, true_frames, pred_atoms, true_atoms, atom_mask, residue_types, swap_flags):
     dma = pltpu.SemaphoreType.DMA
     blocks = ny * KEPT // FB
+    tiles = -(-nx // 2 * ATOMS // COLS)
     ins = (
         pred_frames, true_frames, pred_atoms, true_atoms, atom_mask.reshape(1, ATOMS),
         residue_types.reshape(1, RESIDUES), swap_flags.reshape(1, RESIDUES), tables(),
     )
     packed = pl.pallas_call(
-        functools.partial(kernel, nx, ny),
+        functools.partial(kernel, nx, ny, tiles),
         out_shape=pltpu.VMEM((8, COLS), F32),
         in_specs=[pl.BlockSpec(memory_space=pl.ANY)] * len(ins),
         out_specs=pl.BlockSpec(memory_space=pltpu.VMEM),
@@ -375,16 +379,17 @@
             pltpu.VMEM((ny, 16, FRAMES), F32),
             pltpu.VMEM((nx, 8, COLS), F32),
             pltpu.VMEM((blocks, 3 * FB, DEPTH), BF16),
-            pltpu.VMEM((nx, DEPTH, COLS), BF16),
+            pltpu.VMEM((2 * tiles, DEPTH, COLS), BF16),
             pltpu.VMEM((ny * KEPT, 128), F32),
-            pltpu.VMEM((nx, 8, COLS), F32),
+            pltpu.VMEM((8, tiles * COLS), F32),
+            pltpu.VMEM((8, tiles * COLS), F32),
             pltpu.VMEM((nx, 1, COLS), F32),
             pltpu.VMEM((nx, 1, COLS), F32),
             pltpu.VMEM((ny, 2, 128), F32),
             pltpu.VMEM((ny, 2, 128), F32),
             pltpu.VMEM((nx, 2, 128), F32),
             pltpu.VMEM((ny, 1, 128), F32),
-            dma((len(ins),)), dma((6,)), dma((ny,)), dma((3,)), dma((1,)), dma((1,)), dma((2,)),
+            dma((len(ins),)), dma((6,)), dma((ny,)), dma((2,)), dma((1,)), dma((1,)), dma((2,)),
         ],
         compiler_params=pltpu.CompilerParams(collective_id=0, has_side_effects=True),
         name="fape",

time: 34.5 us -> 34.2 us (level)
  no operation moved by 1% of the time
where the time goes in v3:
time: 34.2 us; the launch traced here: 34.1 us
  Pallas kernels  31.9 us (93%)
  local copies, waits for them, and re-layouts  1.59 us (5%)
  between operations  0.64 us (2%)
    pallas_call x1, Pallas kernels, shards(): pl.pallas_call(functools.partial(kernel, nx, ny, tiles), out_shape=pltpu....  31.9 us
    slice x2, local copies, waits for them, and re-layouts, shards(): return (packed[0, :FRAMES], packed[1, :ATOMS], packed[2, :1])  1.08 us

profile of v3, /device:TPU:1, one launch (start us, length us, event | category | flops | bytes accessed | tf_op | source)
XLA Modules:
  0.0 34.1 jit_solution(9866510990324181958)
XLA Ops:
  0.6 31.9 %fape.1 = f32[8,256]{1,0:T(8,128)S(1)} custom-call(f32[12,128]{1,0:T(8,128)} %pf_hbm.1, f32[12,128]{1,0:T(8,128)} %tf_hbm.1, f32[3,224]{1,0:T(4,128)} %pa_hbm.1, f32[3,224]{1,0:T(4,128)} %ta_hbm.1, s32[1,224]{1,0:T(1,128)} %bitcast.7, s32[1,16]{1,0:T(1,128)} %bitcast.9, s32[1,16]{1,0:T(1,128)} %bitcast.10, bf16[192,384]{1,0:T(8,128)(2,1)} %constant.2.clone.consts_hbm), custom_call_target="tpu_custom_call" | custom-call | tf_op jit(solution)/shard_map/fape/pallas_call | solution.py:371
  32.6 0.5 %slice.11 = f32[1,1]{1,0:T(1,128)} slice(f32[8,256]{1,0:T(8,128)S(1)} %fape.1), slice={[2:3], [0:1]} | slice | bytes 8 | tf_op jit(solution)/shard_map/slice | solution.py:397
  33.1 0.5 %slice_bitcast_fusion = f32[128]{0:T(128)} fusion(f32[8,256]{1,0:T(8,128)S(1)} %fape.1), kind=kLoop, calls=%fused_computation | loop fusion | bytes 1024 | tf_op jit(solution)/shard_map/squeeze | solution.py:397
  33.6 0.6 %slice.10 = f32[1,224]{1,0:T(1,128)} slice(f32[8,256]{1,0:T(8,128)S(1)} %fape.1), slice={[1:2], [0:224]} | slice | bytes 1792 | tf_op jit(solution)/shard_map/slice | solution.py:397

commit v4 on v3

--- a/solution.py
+++ b/solution.py
@@ -89,8 +89,8 @@
     out_ref,
     pf, tf, pa, ta, mask, types, swaps, consts,
     res, frames, atoms, lhs, rhs, acc_f, packed, unpacked,
-    asend, arecv, psend, precv, tsend, usend,
-    in_sem, send_sem, frame_sem, atom_sem, sum_sem, part_sem, total_sems,
+    asend, arecv, psend, precv, totals,
+    in_sem, send_sem, frame_sem, atom_sem, sum_sem, part_sem, total_sem,
 ):
     gx, gy = lax.axis_index("gx"), lax.axis_index("gy")
     nz, nw, part = nx // 2, ny // 2, nx // 2
@@ -135,6 +135,7 @@
     atoms[0] = jnp.zeros((8, COLS), F32)
     acc_f[...] = jnp.zeros_like(acc_f)
     asend[...] = jnp.zeros_like(asend)
+    psend[...] = jnp.zeros_like(psend)
     if part * ATOMS != tiles * COLS:
         packed[...] = jnp.zeros_like(packed)
     for load in loads:
@@ -245,82 +246,92 @@
             sums[k] = sums[k] + clamped.reshape(FB // 8, 8, COLS).sum(axis=0)
         acc_f[pl.ds(start, FB)] += total
 
-    def send_sums(group, sums):
+    def column_rows(sums):
         total = jnp.zeros((1, COLS), F32)
         for t, value in enumerate(sums):
             row = value.sum(axis=0, keepdims=True)
             unpacked[0:1, t * COLS : (t + 1) * COLS] = row
             total = total + row
+        return total
+
+    def send_sums(group, frame_flags):
         for k in range(part):
             j = group * part + k
             asend[j, :, 0:ATOMS] = unpacked[0:1, k * ATOMS : (k + 1) * ATOMS]
-            if j:
-                pltpu.make_async_remote_copy(
-                    asend.at[j], arecv.at[j], send_sem.at[2], sum_sem.at[0], from_x(j), MESH
-                ).start()
-        return total
-
-    def wait_frames(s):
-        all_of(frames.at[s, 0:13], frame_sem.at[s])
-        frame_side(s)
+            asend[j, :, ATOMS : ATOMS + 1] = frame_flags
+        for j in range(max(1, group * part), (group + 1) * part):
+            pltpu.make_async_remote_copy(
+                asend.at[j], arecv.at[j], send_sem.at[2], sum_sem.at[0], from_x(j), MESH
+            ).start()
+
+    def wait_frames(low, high):
+        for s in range(low, high):
+            all_of(frames.at[s, 0:13], frame_sem.at[s])
+        for s in range(low, high):
+            frame_side(s)
 
     near = ny // 2 + 1
     frame_side(0)
     all_of(atoms.at[1:part, 0:7], atom_sem.at[0])
+    wait_frames(1, near)
     atom_side(0)
-    for s in range(1, near):
-        wait_frames(s)
     sums = [jnp.zeros((8, COLS), F32) for _ in range(tiles)]
     for q in range(near * chunks):
         pair_block(q * FB, q, range(tiles), sums)
-    for s in range(near, ny):
-        wait_frames(s)
+    wait_frames(near, ny)
     for q in range(near * chunks, ny * chunks):
         pair_block(q * FB, q, range(tiles), sums)
-    running = send_sums(0, sums)
     all_of(atoms.at[part:nx, 0:7], atom_sem.at[1])
     atom_side(1)
+    flags = frames[0, 12:13]
+    for s in range(1, ny):
+        flags = flags + frames[s, 12:13]
+    flags = jnp.sum(flags, axis=1, keepdims=True)
+    running = column_rows(sums)
+    send_sums(0, flags)
     sums = [jnp.zeros((8, COLS), F32) for _ in range(tiles)]
     for q in range(ny * chunks):
         pair_block(q * FB, q, range(tiles, 2 * tiles), sums)
-    running = running + send_sums(1, sums)
-
-    frame_flags = frames[0, 12:13]
-    for s in range(1, ny):
-        frame_flags = frame_flags + frames[s, 12:13]
-    tsend[0, 0:1] = running[:, :128] + running[:, 128:]
-    tsend[0, 1:2] = frame_flags
-    for j in range(1, nx):
+    running = running + column_rows(sums)
+
+    def hops(jx, jy):
+        dz, dw = near_z[jx // 2], near_w[jy % nw]
+        return min(dz, nz - dz) + min(dw, nw - dw) + 2 * (jy // nw)
+
+    others = sorted(
+        ((jx, jy) for jx in range(nx) for jy in range(ny) if jx or jy), key=lambda j: -hops(*j)
+    )
+
+    def send_total(jx, jy):
+        k = jx * ny + jy
         pltpu.make_async_remote_copy(
-            tsend.at[0], tsend.at[j], send_sem.at[3], total_sems.at[0], to_x(j), MESH
+            totals.at[0:1], totals.at[k : k + 1], send_sem.at[3], total_sem.at[0],
+            {**to_x(jx), **to_y(jy)}, MESH,
         ).start()
+
+    totals[0:1] = running[:, :128] + running[:, 128:]
+    first_sent = len(others) // 2
+    for j in others[:first_sent]:
+        send_total(*j)
+    send_sums(1, flags)
 
     ones = jnp.ones((8, 128), BF16)
     weights = jnp.zeros((1, COLS), F32)
     for j in range(nx):
         weights = weights + atoms[j, 6:7]
-    psend[...] = jnp.zeros_like(psend)
+    weights = jnp.sum(weights, axis=1, keepdims=True)
     for s in range(ny):
         partial = jnp.zeros((8, KEPT), F32)
-        for part in pieces(acc_f[s * KEPT : (s + 1) * KEPT], 3):
-            partial = partial + dot_nt(ones, part.astype(BF16))
-        psend[s, 0:1, 0:KEPT] = partial[0:1]
-        psend[s, 1:2] = weights[:, :128] + weights[:, 128:]
-        if s:
-            pltpu.make_async_remote_copy(
-                psend.at[s], precv.at[s], send_sem.at[4], part_sem.at[0], from_y(s), MESH
-            ).start()
-
-    all_of(tsend.at[1:nx], total_sems.at[0])
-    both = tsend[0]
-    for j in range(1, nx):
-        both = both + tsend[j]
-    usend[0] = both[0:1]
-    for j in range(1, ny):
+        for piece in pieces(acc_f[s * KEPT : (s + 1) * KEPT], 3):
+            partial = partial + dot_nt(ones, piece.astype(BF16))
+        psend[s, :, 0:KEPT] = partial[0:1]
+        psend[s, :, KEPT : KEPT + 1] = weights
+    for s in range(1, ny):
         pltpu.make_async_remote_copy(
-            usend.at[0], usend.at[j], send_sem.at[5], total_sems.at[1], to_y(j), MESH
+            psend.at[s], precv.at[s], send_sem.at[4], part_sem.at[0], from_y(s), MESH
         ).start()
-    frame_count = jnp.sum(both[1:2], axis=1, keepdims=True)
+    for j in others[first_sent:]:
+        send_total(*j)
 
     columns = F32(2 * tiles * ny * COLS)
     rows = F32(nx * ny * KEPT)
@@ -328,12 +339,12 @@
     mine = psend[0]
     for s in range(1, ny):
         mine = mine + precv[s]
-    atom_count = jnp.sum(mine[1:2], axis=1, keepdims=True)
-    least_y = jnp.zeros((1, 128), F32) * mine[0:1] + EPS
+    atom_count = mine[:, KEPT : KEPT + 1]
+    least_y = jnp.zeros((1, 128), F32) * mine + EPS
     least = least_y * lax.rsqrt(least_y)
     own_sum = jnp.zeros((8, FRAMES), F32)
-    for part in pieces(jnp.broadcast_to(mine[0:1, :KEPT], (8, KEPT)), 3):
-        own_sum = own_sum + dot(part.astype(BF16), keep)
+    for piece in pieces(jnp.broadcast_to(mine[:, :KEPT], (8, KEPT)), 3):
+        own_sum = own_sum + dot(piece.astype(BF16), keep)
     out_ref[0:1, 0:FRAMES] = (
         frames[0, 12:13] * (own_sum[0:1] - (columns - atom_count) * least) / atom_count
     )
@@ -341,23 +352,22 @@
     asum = asend[0]
     for j in range(1, nx):
         asum = asum + arecv[j]
+    frame_count = asum[:, ATOMS : ATOMS + 1]
     wide = jnp.concatenate([least, least], axis=1)
     out_ref[1:2, :] = atoms[0, 6:7] * (asum - (rows - frame_count) * wide) / frame_count
     pairs = frame_count * atom_count
 
-    all_of(usend.at[1:ny], total_sems.at[1])
-    both = usend[0]
-    for j in range(1, ny):
-        both = both + usend[j]
-    numerator = jnp.sum(both, axis=1, keepdims=True)
+    all_of(totals.at[1 : nx * ny], total_sem.at[0])
+    numerator = jnp.sum(
+        jnp.sum(totals[...], axis=0, keepdims=True), axis=1, keepdims=True
+    )
     out_ref[2:3, 0:128] = (numerator - least * (rows * columns - pairs)) / pairs
 
     all_of(frames.at[1:ny, 0:13], send_sem.at[0])
     all_of(atoms.at[1:nx, 0:7], send_sem.at[1])
     all_of(arecv.at[1:nx], send_sem.at[2])
-    all_of(tsend.at[1:nx], send_sem.at[3])
+    all_of(totals.at[1 : nx * ny], send_sem.at[3])
     all_of(precv.at[1:ny], send_sem.at[4])
-    all_of(usend.at[1:ny], send_sem.at[5])
 
 
 def shards(nx, ny, pred_frames, true_frames, pred_atoms, true_atoms, atom_mask, residue_types, swap_flags):
@@ -385,11 +395,10 @@
             pltpu.VMEM((8, tiles * COLS), F32),
             pltpu.VMEM((nx, 1, COLS), F32),
             pltpu.VMEM((nx, 1, COLS), F32),
-            pltpu.VMEM((ny, 2, 128), F32),
-            pltpu.VMEM((ny, 2, 128), F32),
-            pltpu.VMEM((nx, 2, 128), F32),
             pltpu.VMEM((ny, 1, 128), F32),
-            dma((len(ins),)), dma((6,)), dma((ny,)), dma((2,)), dma((1,)), dma((1,)), dma((2,)),
+            pltpu.VMEM((ny, 1, 128), F32),
+            pltpu.VMEM((nx * ny, 128), F32),
+            dma((len(ins),)), dma((5,)), dma((ny,)), dma((2,)), dma((1,)), dma((1,)), dma((1,)),
         ],
         compiler_params=pltpu.CompilerParams(collective_id=0, has_side_effects=True),
         name="fape",

time: 34.2 us -> 31 us (0.906)
  Pallas kernels: 31.9 us -> 28.7 us
    pallas_call x1, Pallas kernels: 31.9 us -> 28.7 us  [shards(): pl.pallas_call(functools.partial(kernel, nx, ny, tiles), out_shape=pltpu....]
where the time goes in v4:
time: 31 us; the launch traced here: 30.9 us
  Pallas kernels  28.7 us (93%)
  local copies, waits for them, and re-layouts  1.59 us (5%)
  between operations  0.64 us (2%)
    pallas_call x1, Pallas kernels, shards(): pl.pallas_call(functools.partial(kernel, nx, ny, tiles), out_shape=pltpu....  28.7 us
    slice x2, local copies, waits for them, and re-layouts, shards(): return (packed[0, :FRAMES], packed[1, :ATOMS], packed[2, :1])  1.08 us

profile of v4, /device:TPU:1, one launch (start us, length us, event | category | flops | bytes accessed | tf_op | source)
XLA Modules:
  0.0 30.9 jit_solution(13172937226407603309)
XLA Ops:
  0.6 28.7 %fape.1 = f32[8,256]{1,0:T(8,128)S(1)} custom-call(f32[12,128]{1,0:T(8,128)} %pf_hbm.1, f32[12,128]{1,0:T(8,128)} %tf_hbm.1, f32[3,224]{1,0:T(4,128)} %pa_hbm.1, f32[3,224]{1,0:T(4,128)} %ta_hbm.1, s32[1,224]{1,0:T(1,128)} %bitcast.7, s32[1,16]{1,0:T(1,128)} %bitcast.9, s32[1,16]{1,0:T(1,128)} %bitcast.10, bf16[192,384]{1,0:T(8,128)(2,1)} %constant.2.clone.consts_hbm), custom_call_target="tpu_custom_call" | custom-call | tf_op jit(solution)/shard_map/fape/pallas_call | solution.py:381
  29.3 0.5 %slice.11 = f32[1,1]{1,0:T(1,128)} slice(f32[8,256]{1,0:T(8,128)S(1)} %fape.1), slice={[2:3], [0:1]} | slice | bytes 8 | tf_op jit(solution)/shard_map/slice | solution.py:406
  29.8 0.5 %slice_bitcast_fusion = f32[128]{0:T(128)} fusion(f32[8,256]{1,0:T(8,128)S(1)} %fape.1), kind=kLoop, calls=%fused_computation | loop fusion | bytes 1024 | tf_op jit(solution)/shard_map/squeeze | solution.py:406
  30.3 0.6 %slice.10 = f32[1,224]{1,0:T(1,128)} slice(f32[8,256]{1,0:T(8,128)S(1)} %fape.1), slice={[1:2], [0:224]} | slice | bytes 1792 | tf_op jit(solution)/shard_map/slice | solution.py:406

commit v5 on v4

--- a/solution.py
+++ b/solution.py
@@ -88,7 +88,7 @@
     pf_hbm, tf_hbm, pa_hbm, ta_hbm, mask_hbm, type_hbm, swap_hbm, consts_hbm,
     out_ref,
     pf, tf, pa, ta, mask, types, swaps, consts,
-    res, frames, atoms, lhs, rhs, acc_f, packed, unpacked,
+    res, frames, atoms, lhs, rhs, acc_f, acc_c, packed, unpacked,
     asend, arecv, psend, precv, totals,
     in_sem, send_sem, frame_sem, atom_sem, sum_sem, part_sem, total_sem,
 ):
@@ -134,6 +134,7 @@
     res[...] = jnp.zeros_like(res)
     atoms[0] = jnp.zeros((8, COLS), F32)
     acc_f[...] = jnp.zeros_like(acc_f)
+    acc_c[...] = jnp.zeros_like(acc_c)
     asend[...] = jnp.zeros_like(asend)
     psend[...] = jnp.zeros_like(psend)
     if part * ATOMS != tiles * COLS:
@@ -198,9 +199,16 @@
 
     pl.semaphore_wait(barrier, nx - 1 + ny - 1)
 
+    if nx == 16:
+        atom_tiers, tile_tiers = (0, 6, 8, 14, 16), (0, 5, 7, 12, 14)
+    else:
+        atom_tiers, tile_tiers = (0, part, part, nx, nx), (0, tiles, tiles, 2 * tiles, 2 * tiles)
+    frame_tiers = (0, 3, 5, 7, 8) if ny == 8 else (0, 1, nw, ny, ny)
+    tier_of = [k for k in range(4) for _ in range(atom_tiers[k], atom_tiers[k + 1])]
+
     def send_atoms(j):
         pltpu.make_async_remote_copy(
-            atoms.at[0, 0:7], atoms.at[j, 0:7], send_sem.at[1], atom_sem.at[j // part],
+            atoms.at[0, 0:7], atoms.at[j, 0:7], send_sem.at[1], atom_sem.at[tier_of[j]],
             to_x(j), MESH,
         ).start()
 
@@ -226,73 +234,87 @@
                     q * FB : (q + 1) * FB, c * 128 : c * 128 + DEPTH
                 ]
 
-    def atom_side(group):
-        for k in range(part):
-            packed[:, k * ATOMS : (k + 1) * ATOMS] = atoms[group * part + k, :, 0:ATOMS]
-        split = jnp.concatenate(pieces(packed[...], 3), axis=0).astype(BF16)
+    def atom_side(tier):
+        low, high = tile_tiers[tier : tier + 2]
+        for j in range(*atom_tiers[tier : tier + 2]):
+            k = j % part * ATOMS
+            packed[j // part, :, k : k + ATOMS] = atoms[j, :, 0:ATOMS]
+        group, first = low // tiles, low % tiles
+        lanes = packed[group, :, first * COLS : (first + high - low) * COLS]
+        split = jnp.concatenate(pieces(lanes, 3), axis=0).astype(BF16)
         side = dot(apick, split).astype(BF16)
-        for t in range(tiles):
-            rhs[group * tiles + t] = side[:, t * COLS : (t + 1) * COLS]
-
-    def pair_block(start, q, segments, sums):
-        total = jnp.zeros((FB, 128), F32)
-        for k, j in enumerate(segments):
-            e = dot(lhs[q], rhs[j])
-            e0, e1, e2 = e[:FB], e[FB : 2 * FB], e[2 * FB :]
-            y = jnp.minimum((e0 * e0 + e1 * e1) + (e2 * e2 + EPS), 1.0)
-            clamped = y * lax.rsqrt(y)
-            side = clamped[:, :128] + clamped[:, 128:]
-            total = side if k == 0 else total + side
-            sums[k] = sums[k] + clamped.reshape(FB // 8, 8, COLS).sum(axis=0)
-        acc_f[pl.ds(start, FB)] += total
-
-    def column_rows(sums):
+        for t in range(high - low):
+            rhs[low + t] = side[:, t * COLS : (t + 1) * COLS]
+
+    def pairs_of(blocks):
+        for low, high, first, last in blocks:
+            sums = [acc_c[t] for t in range(first, last)]
+            for q in range(low * chunks, high * chunks):
+                total = jnp.zeros((FB, 128), F32)
+                for k in range(last - first):
+                    e = dot(lhs[q], rhs[first + k])
+                    e0, e1, e2 = e[:FB], e[FB : 2 * FB], e[2 * FB :]
+                    y = jnp.minimum((e0 * e0 + e1 * e1) + (e2 * e2 + EPS), 1.0)
+                    clamped = y * lax.rsqrt(y)
+                    side = clamped[:, :128] + clamped[:, 128:]
+                    total = side if k == 0 else total + side
+                    sums[k] = sums[k] + clamped.reshape(FB // 8, 8, COLS).sum(axis=0)
+                acc_f[q * FB : (q + 1) * FB] += total
+            for k, value in enumerate(sums):
+                acc_c[first + k] = value
+
+    def column_rows():
         total = jnp.zeros((1, COLS), F32)
-        for t, value in enumerate(sums):
-            row = value.sum(axis=0, keepdims=True)
-            unpacked[0:1, t * COLS : (t + 1) * COLS] = row
+        for t in range(2 * tiles):
+            row = acc_c[t].sum(axis=0, keepdims=True)
+            k = t % tiles * COLS
+            unpacked[t // tiles : t // tiles + 1, k : k + COLS] = row
             total = total + row
         return total
 
     def send_sums(group, frame_flags):
         for k in range(part):
             j = group * part + k
-            asend[j, :, 0:ATOMS] = unpacked[0:1, k * ATOMS : (k + 1) * ATOMS]
+            asend[j, :, 0:ATOMS] = unpacked[group : group + 1, k * ATOMS : (k + 1) * ATOMS]
             asend[j, :, ATOMS : ATOMS + 1] = frame_flags
         for j in range(max(1, group * part), (group + 1) * part):
             pltpu.make_async_remote_copy(
                 asend.at[j], arecv.at[j], send_sem.at[2], sum_sem.at[0], from_x(j), MESH
             ).start()
 
-    def wait_frames(low, high):
+    held = []
+    for tier in range(4):
+        first, last = tile_tiers[tier : tier + 2]
+        low, high = frame_tiers[tier : tier + 2]
+        slots = atom_tiers[tier : tier + 2]
+        if tier == 0:
+            frame_side(0)
+        if max(1, slots[0]) < slots[1]:
+            all_of(atoms.at[max(1, slots[0]) : slots[1], 0:7], atom_sem.at[tier])
+        for s in range(max(1, low), high):
+            all_of(frames.at[s, 0:13], frame_sem.at[s])
+        for s in range(max(1, low), high):
+            frame_side(s)
+        if first < last:
+            atom_side(tier)
+        pairs_of(held)
+        blocks = []
+        if first < last:
+            blocks.append((0, low, first, last))
         for s in range(low, high):
-            all_of(frames.at[s, 0:13], frame_sem.at[s])
-        for s in range(low, high):
-            frame_side(s)
-
-    near = ny // 2 + 1
-    frame_side(0)
-    all_of(atoms.at[1:part, 0:7], atom_sem.at[0])
-    wait_frames(1, near)
-    atom_side(0)
-    sums = [jnp.zeros((8, COLS), F32) for _ in range(tiles)]
-    for q in range(near * chunks):
-        pair_block(q * FB, q, range(tiles), sums)
-    wait_frames(near, ny)
-    for q in range(near * chunks, ny * chunks):
-        pair_block(q * FB, q, range(tiles), sums)
-    all_of(atoms.at[part:nx, 0:7], atom_sem.at[1])
-    atom_side(1)
+            for group in range(2):
+                bounds = max(0, group * tiles), min(last, (group + 1) * tiles)
+                if bounds[0] < bounds[1]:
+                    blocks.append((s, s + 1, *bounds))
+        blocks = [b for b in blocks if b[0] < b[1]]
+        hold = 1 if tier < 3 else 0
+        held = blocks[len(blocks) - hold :]
+        pairs_of(blocks[: len(blocks) - hold])
     flags = frames[0, 12:13]
     for s in range(1, ny):
         flags = flags + frames[s, 12:13]
     flags = jnp.sum(flags, axis=1, keepdims=True)
-    running = column_rows(sums)
-    send_sums(0, flags)
-    sums = [jnp.zeros((8, COLS), F32) for _ in range(tiles)]
-    for q in range(ny * chunks):
-        pair_block(q * FB, q, range(tiles, 2 * tiles), sums)
-    running = running + column_rows(sums)
+    running = column_rows()
 
     def hops(jx, jy):
         dz, dw = near_z[jx // 2], near_w[jy % nw]
@@ -313,6 +335,7 @@
     first_sent = len(others) // 2
     for j in others[:first_sent]:
         send_total(*j)
+    send_sums(0, flags)
     send_sums(1, flags)
 
     ones = jnp.ones((8, 128), BF16)
@@ -391,14 +414,15 @@
             pltpu.VMEM((blocks, 3 * FB, DEPTH), BF16),
             pltpu.VMEM((2 * tiles, DEPTH, COLS), BF16),
             pltpu.VMEM((ny * KEPT, 128), F32),
-            pltpu.VMEM((8, tiles * COLS), F32),
+            pltpu.VMEM((2 * tiles, 8, COLS), F32),
+            pltpu.VMEM((2, 8, tiles * COLS), F32),
             pltpu.VMEM((8, tiles * COLS), F32),
             pltpu.VMEM((nx, 1, COLS), F32),
             pltpu.VMEM((nx, 1, COLS), F32),
             pltpu.VMEM((ny, 1, 128), F32),
             pltpu.VMEM((ny, 1, 128), F32),
             pltpu.VMEM((nx * ny, 128), F32),
-            dma((len(ins),)), dma((5,)), dma((ny,)), dma((2,)), dma((1,)), dma((1,)), dma((1,)),
+            dma((len(ins),)), dma((5,)), dma((ny,)), dma((4,)), dma((1,)), dma((1,)), dma((1,)),
         ],
         compiler_params=pltpu.CompilerParams(collective_id=0, has_side_effects=True),
         name="fape",

time: 31 us -> 30.1 us (0.971)
  Pallas kernels: 28.7 us -> 27.8 us
    pallas_call x1, Pallas kernels: 28.7 us -> 27.8 us  [shards(): pl.pallas_call(functools.partial(kernel, nx, ny, tiles), out_shape=pltpu....]
where the time goes in v5:
time: 30.1 us; the launch traced here: 30 us
  Pallas kernels  27.8 us (92%)
  local copies, waits for them, and re-layouts  1.59 us (5%)
  between operations  0.64 us (2%)
    pallas_call x1, Pallas kernels, shards(): pl.pallas_call(functools.partial(kernel, nx, ny, tiles), out_shape=pltpu....  27.8 us
    slice x2, local copies, waits for them, and re-layouts, shards(): return (packed[0, :FRAMES], packed[1, :ATOMS], packed[2, :1])  1.08 us

profile of v5, /device:TPU:1, one launch (start us, length us, event | category | flops | bytes accessed | tf_op | source)
XLA Modules:
  0.0 30.0 jit_solution(5918336603101997262)
XLA Ops:
  0.6 27.8 %fape.1 = f32[8,256]{1,0:T(8,128)S(1)} custom-call(f32[12,128]{1,0:T(8,128)} %pf_hbm.1, f32[12,128]{1,0:T(8,128)} %tf_hbm.1, f32[3,224]{1,0:T(4,128)} %pa_hbm.1, f32[3,224]{1,0:T(4,128)} %ta_hbm.1, s32[1,224]{1,0:T(1,128)} %bitcast.7, s32[1,16]{1,0:T(1,128)} %bitcast.9, s32[1,16]{1,0:T(1,128)} %bitcast.10, bf16[192,384]{1,0:T(8,128)(2,1)} %constant.2.clone.consts_hbm), custom_call_target="tpu_custom_call" | custom-call | tf_op jit(solution)/shard_map/fape/pallas_call | solution.py:404
  28.4 0.5 %slice.11 = f32[1,1]{1,0:T(1,128)} slice(f32[8,256]{1,0:T(8,128)S(1)} %fape.1), slice={[2:3], [0:1]} | slice | bytes 8 | tf_op jit(solution)/shard_map/slice | solution.py:430
  28.9 0.5 %slice_bitcast_fusion = f32[128]{0:T(128)} fusion(f32[8,256]{1,0:T(8,128)S(1)} %fape.1), kind=kLoop, calls=%fused_computation | loop fusion | bytes 1024 | tf_op jit(solution)/shard_map/squeeze | solution.py:430
  29.4 0.6 %slice.10 = f32[1,224]{1,0:T(1,128)} slice(f32[8,256]{1,0:T(8,128)S(1)} %fape.1), slice={[1:2], [0:224]} | slice | bytes 1792 | tf_op jit(solution)/shard_map/slice | solution.py:430

commit v6 on v5

--- a/solution.py
+++ b/solution.py
@@ -98,27 +98,23 @@
     near_z = [0] + [d for k in range(1, nz // 2 + 1) for d in sorted({k, nz - k})]
     near_w = [0] + [d for k in range(1, nw // 2 + 1) for d in sorted({k, nw - k})]
 
+    ahead = [2 * lax.rem(z + d, nz) for d in near_z]
+    behind = [2 * lax.rem(z + nz - d, nz) for d in near_z]
+    ahead_w = [2 * lax.rem(w + d, nw) for d in near_w]
+    behind_w = [2 * lax.rem(w + nw - d, nw) for d in near_w]
+    cores, halves = (core, 1 - core), (half, 1 - half)
+
     def to_x(j):
-        return {"gx": 2 * lax.rem(z + near_z[j // 2], nz) + lax.rem(core + j % 2, 2)}
+        return {"gx": ahead[j // 2] + cores[j % 2]}
 
     def from_x(j):
-        return {"gx": 2 * lax.rem(z + nz - near_z[j // 2], nz) + lax.rem(core + j % 2, 2)}
+        return {"gx": behind[j // 2] + cores[j % 2]}
 
     def to_y(j):
-        return {"gy": 2 * lax.rem(w + near_w[j % nw], nw) + lax.rem(half + j // nw, 2)}
+        return {"gy": ahead_w[j % nw] + halves[j // nw]}
 
     def from_y(j):
-        return {"gy": 2 * lax.rem(w + nw - near_w[j % nw], nw) + lax.rem(half + j // nw, 2)}
-
-    for j in range(nx):
-        atoms[j, 7:8] = jnp.zeros((1, COLS), F32)
-    for j in range(ny):
-        frames[j, 13:16] = jnp.zeros((3, FRAMES), F32)
-    barrier = pltpu.get_barrier_semaphore()
-    for j in range(1, nx):
-        pl.semaphore_signal(barrier, inc=1, device_id=to_x(j), device_id_type=MESH)
-    for j in range(1, ny):
-        pl.semaphore_signal(barrier, inc=1, device_id=to_y(j), device_id_type=MESH)
+        return {"gy": behind_w[j % nw] + halves[j // nw]}
 
     loads = [
         pltpu.make_async_copy(src, dst, in_sem.at[k])
@@ -131,6 +127,16 @@
     ]
     for load in loads:
         load.start()
+    for j in range(nx):
+        atoms[j, 7:8] = jnp.zeros((1, COLS), F32)
+    for j in range(ny):
+        frames[j, 13:16] = jnp.zeros((3, FRAMES), F32)
+    barrier = pltpu.get_barrier_semaphore()
+    for j in range(1, nx):
+        pl.semaphore_signal(barrier, inc=1, device_id=to_x(j), device_id_type=MESH)
+    for j in range(1, ny):
+        pl.semaphore_signal(barrier, inc=1, device_id=to_y(j), device_id_type=MESH)
+
     res[...] = jnp.zeros_like(res)
     atoms[0] = jnp.zeros((8, COLS), F32)
     acc_f[...] = jnp.zeros_like(acc_f)

time: 30.1 us -> 30.1 us (level)
  no operation moved by 1% of the time
where the time goes in v6:
time: 30.1 us; the launch traced here: 30 us
  Pallas kernels  27.8 us (92%)
  local copies, waits for them, and re-layouts  1.59 us (5%)
  between operations  0.64 us (2%)
    pallas_call x1, Pallas kernels, shards(): pl.pallas_call(functools.partial(kernel, nx, ny, tiles), out_shape=pltpu....  27.8 us
    slice x2, local copies, waits for them, and re-layouts, shards(): return (packed[0, :FRAMES], packed[1, :ATOMS], packed[2, :1])  1.08 us

profile of v6, /device:TPU:1, one launch (start us, length us, event | category | flops | bytes accessed | tf_op | source)
XLA Modules:
  0.0 30.0 jit_solution(8845152641922121750)
XLA Ops:
  0.6 27.8 %fape.1 = f32[8,256]{1,0:T(8,128)S(1)} custom-call(f32[12,128]{1,0:T(8,128)} %pf_hbm.1, f32[12,128]{1,0:T(8,128)} %tf_hbm.1, f32[3,224]{1,0:T(4,128)} %pa_hbm.1, f32[3,224]{1,0:T(4,128)} %ta_hbm.1, s32[1,224]{1,0:T(1,128)} %bitcast.7, s32[1,16]{1,0:T(1,128)} %bitcast.9, s32[1,16]{1,0:T(1,128)} %bitcast.10, bf16[192,384]{1,0:T(8,128)(2,1)} %constant.2.clone.consts_hbm), custom_call_target="tpu_custom_call" | custom-call | tf_op jit(solution)/shard_map/fape/pallas_call | solution.py:410
  28.4 0.5 %slice.11 = f32[1,1]{1,0:T(1,128)} slice(f32[8,256]{1,0:T(8,128)S(1)} %fape.1), slice={[2:3], [0:1]} | slice | bytes 8 | tf_op jit(solution)/shard_map/slice | solution.py:436
  28.9 0.5 %slice_bitcast_fusion = f32[128]{0:T(128)} fusion(f32[8,256]{1,0:T(8,128)S(1)} %fape.1), kind=kLoop, calls=%fused_computation | loop fusion | bytes 1024 | tf_op jit(solution)/shard_map/squeeze | solution.py:436
  29.5 0.6 %slice.10 = f32[1,224]{1,0:T(1,128)} slice(f32[8,256]{1,0:T(8,128)S(1)} %fape.1), slice={[1:2], [0:224]} | slice | bytes 1792 | tf_op jit(solution)/shard_map/slice | solution.py:436
